TPU v7x, 512 devices: a whole 4x8x8 slice. The times are simulated.
512 devices in a mesh: blk: 64 (over x, y, core), spec: 8 (over z).
Axes of the slice: x: 4, y: 8, z: 8, core: 2. Of those that a mesh axis runs over, the one named last changes fastest.
Arguments:
- spectrum: float32 [32, 24, 65536], P('spec', None, 'blk'), may hold values from 0.05 to 2
- depths: float32 [65536], P('blk'), may hold values from 5 to 4000
- currents: float32 [2, 65536], P(None, 'blk'), may hold values from -4 to 4
- slopes: float32 [2, 65536], P(None, 'blk'), may hold values from -0.12 to 0.12
- wind_speed: float32 [2, 65536], P(None, 'blk'), may hold values from -40 to 40
- wet_mask: int32 [65536], P('blk'), may hold values 0 or 1
- face_owner: int32 [4096, 1], P('blk'), may hold values from 0 to 63, as said below
- face_block: int32 [4096], P('blk'), may hold values from 0 to 15
- freq_weights: bfloat16 [2, 32, 32], replicated, may hold values from 0.0049743652 to 0.079589844
- angle_weights: bfloat16 [2, 2, 24, 24], replicated, may hold values from 0.0049743652 to 0.099609375
- transfer_rate: float32 [32], replicated, may hold values from 0.05 to 0.3
Outputs:
- next_spectrum: float32 [32, 24, 65536], P('spec', None, 'blk')
Inputs may be any that keep to these rules, and one draw needn't show every extreme that they name: `face_owner`: face i of one device is side i % 4 (west, east, south, north) of its block i // 4. Of the 64 rows of one device, 32 name another index and the rest name the device itself; no other index is named more than 2 times in those rows, and one is named exactly 2 times.
All inputs are finite; a program needn't handle non-finite values. No bound on the sum of `wet_mask` on one device may be relied on, other than what follows from the above.
Results may differ from a plain program's by a relative error of at most 0.0011.
The roundings to bfloat16 on the way count: a program that leaves them out, or rounds other values in their place, can miss the bound.
Values may be sent and summed in bfloat16 or wider, within the bound.
A program may use at most 64 MiB of HBM per device.

v0:
```python
import math

import jax
import jax.numpy as jnp
from jax import lax
from jax.sharding import PartitionSpec as P

TILE = 8


GRAVITY = 9.81
TIME_STEP = 200.0
CELL_SIZE = 5500.0
LOWEST_FREQ = 0.0418
FREQ_GROWTH = 1.1
WIND_GROWTH = 0.0003
TURN_LIMIT = 0.9


def dispersion(radian_freq, water_depth):
    deep_kh = radian_freq * radian_freq / GRAVITY * water_depth
    wave_kh = deep_kh / jnp.sqrt(jnp.tanh(deep_kh))
    decay_two = jnp.exp(-2.0 * wave_kh)
    denom_term = 1.0 - decay_two * decay_two
    shoal_ratio = 4.0 * wave_kh * decay_two / denom_term
    phase_speed = radian_freq * water_depth / wave_kh
    group_speed = 0.5 * (1.0 + shoal_ratio) * phase_speed
    turn_factor = 2.0 * radian_freq * decay_two / denom_term
    return (phase_speed, group_speed, turn_factor)


def courants(radian_freq, angle_values, water_depth, current_xy, slope_xy, wet_float):
    freq_column = radian_freq[:, None, None, None, None]
    phase_speed, group_speed, turn_factor = dispersion(freq_column, water_depth[None, None])
    cosine = jnp.cos(angle_values)[None, :, None, None, None]
    sine = jnp.sin(angle_values)[None, :, None, None, None]
    grid_ratio = TIME_STEP / CELL_SIZE
    cour_x = (group_speed * cosine + current_xy[0][None, None]) * grid_ratio * wet_float[None, None]
    cour_y = (group_speed * sine + current_xy[1][None, None]) * grid_ratio * wet_float[None, None]
    angle_step = 2.0 * math.pi / angle_values.shape[0]
    turning = (
        turn_factor
        * (sine * slope_xy[0][None, None] - cosine * slope_xy[1][None, None])
        * (TIME_STEP / angle_step)
    )
    cour_turn = jnp.clip(turning, -TURN_LIMIT, TURN_LIMIT)
    return (phase_speed, cour_x, cour_y, cour_turn)


def edge_fluxes(wave_field, cour_x, cour_y):
    west_side = jnp.maximum(-cour_x[..., :, 0], 0.0) * wave_field[..., :, 0]
    east_side = jnp.maximum(cour_x[..., :, -1], 0.0) * wave_field[..., :, -1]
    south_side = jnp.maximum(-cour_y[..., 0, :], 0.0) * wave_field[..., 0, :]
    north_side = jnp.maximum(cour_y[..., -1, :], 0.0) * wave_field[..., -1, :]
    return jnp.stack([west_side, east_side, south_side, north_side], axis=3)


def transported(wave_field, cour_x, cour_y, cour_turn, inflow):
    tile_side = wave_field.shape[-1]
    rightward = jnp.maximum(cour_x, 0.0) * wave_field
    leftward = jnp.maximum(-cour_x, 0.0) * wave_field
    upward = jnp.maximum(cour_y, 0.0) * wave_field
    downward = jnp.maximum(-cour_y, 0.0) * wave_field
    lead_pads = [(0, 0)] * 3
    from_x = jnp.pad(rightward[..., :, :-1], lead_pads + [(0, 0), (1, 0)]) + jnp.pad(
        leftward[..., :, 1:], lead_pads + [(0, 0), (0, 1)]
    )
    from_y = jnp.pad(upward[..., :-1, :], lead_pads + [(1, 0), (0, 0)]) + jnp.pad(
        downward[..., 1:, :], lead_pads + [(0, 1), (0, 0)]
    )
    from_turn = jnp.roll(jnp.maximum(cour_turn, 0.0) * wave_field, 1, axis=1) + jnp.roll(
        jnp.maximum(-cour_turn, 0.0) * wave_field, -1, axis=1
    )
    ghost_x = jnp.pad(inflow[:, :, :, 0, :, None], lead_pads + [(0, 0), (0, tile_side - 1)])
    ghost_x = ghost_x + jnp.pad(
        inflow[:, :, :, 1, :, None], lead_pads + [(0, 0), (tile_side - 1, 0)]
    )
    ghost_y = jnp.pad(inflow[:, :, :, 2, None, :], lead_pads + [(0, tile_side - 1), (0, 0)])
    ghost_y = ghost_y + jnp.pad(
        inflow[:, :, :, 3, None, :], lead_pads + [(tile_side - 1, 0), (0, 0)]
    )
    outflow = (jnp.abs(cour_x) + jnp.abs(cour_y) + jnp.abs(cour_turn)) * wave_field
    return wave_field - outflow + from_x + from_y + from_turn + ghost_x + ghost_y


def nonlinear(levels, freq_weights, angle_weights, transfer_rate):
    levels_wide = levels.astype(jnp.float32)
    shifted_plus = jnp.einsum(
        "gf,fdq->gdq", freq_weights[0], levels, preferred_element_type=jnp.float32
    ).astype(jnp.bfloat16)
    shifted_minus = jnp.einsum(
        "gf,fdq->gdq", freq_weights[1], levels, preferred_element_type=jnp.float32
    ).astype(jnp.bfloat16)
    rate_column = transfer_rate[:, None, None]
    delta_list = []
    for mirror in range(2):
        image_plus = jnp.einsum(
            "ed,gdq->geq",
            angle_weights[mirror, 0],
            shifted_plus,
            preferred_element_type=jnp.float32,
        )
        image_minus = jnp.einsum(
            "ed,gdq->geq",
            angle_weights[mirror, 1],
            shifted_minus,
            preferred_element_type=jnp.float32,
        )
        delta_list.append(
            rate_column
            * (
                levels_wide * levels_wide * (image_plus + image_minus)
                - 2.0 * levels_wide * image_plus * image_minus
            )
        )
    low_first = delta_list[0].astype(jnp.bfloat16)
    low_second = delta_list[1].astype(jnp.bfloat16)
    back_plus = (
        jnp.einsum(
            "ed,geq->gdq", angle_weights[0, 0], low_first, preferred_element_type=jnp.float32
        )
        + jnp.einsum(
            "ed,geq->gdq", angle_weights[1, 0], low_second, preferred_element_type=jnp.float32
        )
    ).astype(jnp.bfloat16)
    back_minus = (
        jnp.einsum(
            "ed,geq->gdq", angle_weights[0, 1], low_first, preferred_element_type=jnp.float32
        )
        + jnp.einsum(
            "ed,geq->gdq", angle_weights[1, 1], low_second, preferred_element_type=jnp.float32
        )
    ).astype(jnp.bfloat16)
    spread_plus = jnp.einsum(
        "gf,gdq->fdq", freq_weights[0], back_plus, preferred_element_type=jnp.float32
    )
    spread_minus = jnp.einsum(
        "gf,gdq->fdq", freq_weights[1], back_minus, preferred_element_type=jnp.float32
    )
    return -2.0 * (delta_list[0] + delta_list[1]) + spread_plus + spread_minus


def shards(
    spectrum,
    depths,
    currents,
    slopes,
    wind_speed,
    wet_mask,
    face_owner,
    face_block,
    freq_weights,
    angle_weights,
    transfer_rate,
):
    freq_local, angle_count, point_count = spectrum.shape
    block_count = point_count // (TILE * TILE)
    group_count = lax.axis_size("spec")
    peer_count = lax.axis_size("blk")
    my_index = lax.axis_index("blk")
    face_count = face_block.shape[0]
    remote_total = face_count // 2
    capacity = max(2, (remote_total + peer_count - 2) // (peer_count - 1))
    first_freq = lax.axis_index("spec") * freq_local
    freq_index = (first_freq + jnp.arange(freq_local, dtype=jnp.int32)).astype(jnp.float32)
    radian_freq = 2.0 * math.pi * LOWEST_FREQ * jnp.power(jnp.float32(FREQ_GROWTH), freq_index)
    angle_values = jnp.arange(angle_count, dtype=jnp.int32).astype(jnp.float32) * (
        2.0 * math.pi / angle_count
    )
    wet_float = wet_mask.astype(jnp.float32)
    wave_field = spectrum.reshape(freq_local, angle_count, block_count, TILE, TILE)
    phase_speed, cour_x, cour_y, cour_turn = courants(
        radian_freq,
        angle_values,
        depths.reshape(block_count, TILE, TILE),
        currents.reshape(2, block_count, TILE, TILE),
        slopes.reshape(2, block_count, TILE, TILE),
        wet_float.reshape(block_count, TILE, TILE),
    )
    edges = edge_fluxes(wave_field, cour_x, cour_y)
    edge_rows = edges.transpose(2, 3, 0, 1, 4).reshape(
        block_count * 4, freq_local * angle_count * TILE
    )
    owners = face_owner[:, 0]
    face_sides = jnp.arange(face_count, dtype=jnp.int32) % 4
    wanted_ids = face_block * 4 + jnp.bitwise_xor(face_sides, 1)
    remote_face = (owners != my_index).astype(jnp.int32)
    peer_onehot = (owners[:, None] == jnp.arange(peer_count, dtype=jnp.int32)[None, :]).astype(
        jnp.int32
    ) * remote_face[:, None]
    earlier = jnp.cumsum(peer_onehot, axis=0) - peer_onehot
    slot_ranks = jnp.sum(earlier * peer_onehot, axis=1)
    slot_range = jnp.arange(capacity, dtype=jnp.int32)
    slot_onehot = (slot_ranks[:, None] == slot_range[None, :]).astype(jnp.int32)
    requests = jnp.sum(
        peer_onehot[:, :, None] * (slot_onehot * wanted_ids[:, None])[:, None, :], axis=0
    )
    located = jnp.take(
        edge_rows, lax.all_to_all(requests, "blk", split_axis=0, concat_axis=0, tiled=True), axis=0
    )
    replies = lax.all_to_all(located, "blk", split_axis=0, concat_axis=0, tiled=True)
    remote_index = jnp.where(remote_face > 0, owners * capacity + slot_ranks, 0)
    remote_rows = jnp.take(replies.reshape(peer_count * capacity, -1), remote_index, axis=0)
    local_rows = jnp.take(edge_rows, wanted_ids, axis=0)
    inflow_rows = jnp.where(remote_face[:, None] > 0, remote_rows, local_rows)
    inflow = inflow_rows.reshape(block_count, 4, freq_local, angle_count, TILE).transpose(
        2, 3, 0, 1, 4
    )
    moved = transported(wave_field, cour_x, cour_y, cour_turn, inflow).reshape(
        freq_local, angle_count, point_count
    )
    levels = moved.astype(jnp.bfloat16).reshape(
        freq_local, angle_count, group_count, point_count // group_count
    )
    result = nonlinear(
        lax.all_to_all(levels, "spec", split_axis=2, concat_axis=0, tiled=True)[:, :, 0, :],
        freq_weights,
        angle_weights,
        transfer_rate,
    )
    item_width = result.shape[2]
    split_rows = result.reshape(group_count, freq_local, angle_count, item_width)
    returned = lax.all_to_all(split_rows, "spec", split_axis=0, concat_axis=0, tiled=True)
    transfer = returned.transpose(1, 2, 0, 3).reshape(freq_local, angle_count, point_count)
    along_wind = (
        wind_speed[0][None, None, :] * jnp.cos(angle_values)[None, :, None]
        + wind_speed[1][None, None, :] * jnp.sin(angle_values)[None, :, None]
    )
    phase_flat = phase_speed.reshape(freq_local, 1, point_count)
    growth = (
        TIME_STEP
        * WIND_GROWTH
        * radian_freq[:, None, None]
        * jnp.maximum(along_wind / phase_flat - 1.0, 0.0)
    )
    return wet_float[None, None, :] * (moved + transfer + growth * moved)


def solution(mesh):
    in_specs = (
        P("spec", None, "blk"),
        P("blk"),
        P(None, "blk"),
        P(None, "blk"),
        P(None, "blk"),
        P("blk"),
        P("blk", None),
        P("blk"),
        P(),
        P(),
        P(),
    )
    out_specs = P("spec", None, "blk")
    return jax.shard_map(shards, mesh=mesh, in_specs=in_specs, out_specs=out_specs, check_vma=False)
```

profile of v0, /device:TPU:6, one launch (start us, length us, event | category | flops | bytes accessed | tf_op | source)
XLA Modules:
  0.0 151.9 jit_solution(5503527234569175041)
XLA Ops:
  0.0 1.2 compare_reduce_fusion
  1.2 0.7 fusion.63
  2.0 0.8 fusion.62
  2.9 1.2 compare_and_fusion
  4.2 0.7 copy.142
  4.9 11.0 %all-to-all-start = ((s32[64,1,2]{2,1,0:T(1,128)}), s32[64,1,2]{2,1,0:T(1,128)}, u32[]{:S(2)}, u32[]{:S(2)}) async-start(s32[64,1,2]{2,1,0:T(1,128)} %copy.142), calls=%async_computation | async-start | bytes 65536 | tf_op jit(solution)/shard_map/all_to_all | solution.py:199
  17.2 0.8 mul.516
  18.4 0.8 slice_reduce_fusion.1
  19.5 0.7 broadcast_multiply_fusion
  20.3 1.6 %copy.138 = f32[4,24,1024]{1,2,0:T(8,128)S(1)} copy(f32[4,24,1024]{2,1,0:T(8,128)} %param.11) | data formatting | bytes 786432 | tf_op args[0]
  21.9 1.0 add_multiply_fusion.1
  23.0 1.4 copy-done
  24.4 1.3 slice_multiply_fusion.7
  25.7 0.9 slice_multiply_fusion.5
  27.2 0.7 mul.548
  27.9 0.7 mul.552
  28.8 1.2 multiply_subtract_fusion.1
  30.0 2.4 %maximum_multiply_fusion.1 = (f32[4,24,16,8,8]{1,4,3,2,0:T(8,128)}, f32[4,24,16,8,8]{1,4,3,2,0:T(8,128)}) fusion(f32[4,24,16,8,8]{1,4,3,2,0:T(8,128)S(1)} %bitcast.143, f32[24,16,8,8]{0,3,2,1:T(8,128)S(1)} %multiply_subtract_fusion.1, f32[4,16,8,8]{3,2,1,0:T(8,128)S(1)} %copy.141), kind=kLoop, calls=%fused_computation.17 | loop fusion | flops 786432 | bytes 1294336 | tf_op jit(solution)/shard_map/mul | solution.py:71
  32.5 1.1 maximum_bitcast_fusion
  33.6 3.2 %copy.145 = f32[16,4,4,24,8]{4,3,2,1,0:T(8,128)} copy(f32[16,4,4,24,8]{3,4,1,0,2:T(8,128)} %maximum_bitcast_fusion) | data formatting | bytes 393216 | tf_op jit(solution)/shard_map/transpose | solution.py:181
  36.8 3.4 %reshape.422 = f32[64,768]{1,0:T(8,128)S(1)} reshape(f32[16,4,4,24,8]{4,3,2,1,0:T(8,128)} %copy.145) | data formatting | bytes 393216 | tf_op jit(solution)/shard_map/reshape | solution.py:181
  40.2 0.7 gather_fusion.2
  40.9 3.4 %gather.20 = f32[16,4,4,24,8]{4,3,2,1,0:T(8,128)} reshape(f32[64,768]{1,0:T(8,128)S(1)} %gather_fusion.2) | data formatting | bytes 393216 | tf_op jit(solution)/shard_map/jit(_take)/gather | solution.py:204
  44.2 3.2 %copy.149 = f32[16,4,4,24,8]{3,4,1,0,2:T(8,128)} copy(f32[16,4,4,24,8]{4,3,2,1,0:T(8,128)} %gather.20) | data formatting | bytes 393216 | tf_op jit(solution)/shard_map/jit(_take)/gather | solution.py:204
  48.3 3.7 %slice.162 = f32[4,1,16,8,8]{1,4,3,2,0:T(8,128)} slice(f32[4,24,16,8,8]{1,4,3,2,0:T(8,128)} %get-tuple-element.23), slice={[0:4], [23:24], [0:16], [0:8], [0:8]} | slice | bytes 32768 | tf_op jit(solution)/shard_map/jit(_roll_static)/slice | solution.py:71
  51.9 2.0 %slice.164 = f32[4,23,16,8,8]{1,4,3,2,0:T(8,128)} slice(f32[4,24,16,8,8]{1,4,3,2,0:T(8,128)S(1)} %copy-done.3), slice={[0:4], [1:24], [0:16], [0:8], [0:8]} | slice | bytes 753664 | tf_op jit(solution)/shard_map/jit(_roll_static)/slice | solution.py:71
  54.0 0.8 copy.143
  55.6 1.6 %gather_fusion = f32[128,768]{1,0:T(8,128)} fusion(f32[64,768]{1,0:T(8,128)S(1)} %reshape.422, s32[1024]{0:T(1024)S(1)} %pad_clamp_fusion.2), kind=kCustom, calls=%fused_computation | custom fusion | bytes 786944 | tf_op jit(solution)/shard_map/jit(_take)/gather | solution.py:198
  57.1 1.2 reshape.428
  58.3 0.7 copy.144
  59.0 1.0 broadcast_select_fusion
  60.0 10.5 %all-to-all-start.1 = ((f32[64,2,768]{2,1,0:T(2,128)}), f32[64,2,768]{2,1,0:T(2,128)}, u32[]{:S(2)}, u32[]{:S(2)}) async-start(f32[64,2,768]{2,1,0:T(2,128)} %broadcast_select_fusion), calls=%async_computation.1 | async-start | bytes 786432 | tf_op jit(solution)/shard_map/all_to_all | solution.py:201
  70.5 4.4 %slice_multiply_fusion.3 = (f32[4,24,16,7,8]{1,4,3,2,0:T(8,128)}, f32[4,24,16,7,8]{1,4,3,2,0:T(8,128)}) fusion(f32[4,24,16,8,8]{1,4,3,2,0:T(8,128)S(1)} %bitcast.144, f32[4,24,16,8,8]{1,4,3,2,0:T(8,128)} %copy-done.5), kind=kLoop, calls=%fused_computation.24 | loop fusion | flops 430080 | bytes 2064384 | tf_op jit(solution)/shard_map/mul | solution.py:62
  75.0 2.6 %slice_multiply_fusion.1 = (f32[4,24,16,8,7]{1,4,3,2,0:T(8,128)}, f32[4,24,16,8,7]{1,4,3,2,0:T(8,128)}) fusion(f32[4,24,16,8,8]{1,4,3,2,0:T(8,128)S(1)} %bitcast.145, f32[4,24,16,8,8]{1,4,3,2,0:T(8,128)S(1)} %copy-done.1), kind=kLoop, calls=%fused_computation.12 | loop fusion | flops 430080 | bytes 2064384 | tf_op jit(solution)/shard_map/mul | solution.py:60
  77.6 7.0 %all-to-all-done.1 = f32[64,2,768]{2,1,0:T(2,128)} async-done(((f32[64,2,768]{2,1,0:T(2,128)}), f32[64,2,768]{2,1,0:T(2,128)}, u32[]{:S(2)}, u32[]{:S(2)}) %all-to-all-start.1) | async-done | bytes 393248 | tf_op jit(solution)/shard_map/all_to_all | solution.py:201
  84.6 1.3 reshape.423
  85.9 1.5 gather_fusion.1
  87.3 3.8 %gather.18 = f32[16,4,4,24,8]{4,3,2,1,0:T(8,128)} reshape(f32[64,768]{1,0:T(8,128)} %gather_fusion.1) | data formatting | bytes 393216 | tf_op jit(solution)/shard_map/jit(_take)/gather | solution.py:203
  91.2 3.2 %copy.148 = f32[16,4,4,24,8]{3,4,1,0,2:T(8,128)} copy(f32[16,4,4,24,8]{4,3,2,1,0:T(8,128)} %gather.18) | data formatting | bytes 393216 | tf_op jit(solution)/shard_map/jit(_take)/gather | solution.py:203
  94.3 2.0 %select_bitcast_fusion = f32[4,24,16,4,8]{1,4,3,2,0:T(8,128)S(1)} fusion(f32[16,4,4,24,8]{3,4,1,0,2:T(8,128)} %copy.149, f32[16,4,4,24,8]{3,4,1,0,2:T(8,128)} %copy.148, pred[16,4]{1,0:T(8,128)(4,1)S(1)} %copy-done.28, pred[16,4]{1,0:T(8,128)(4,1)S(1)} %broadcast_in_dim.64, pred[16,4]{1,0:T(8,128)(4,1)S(1)} %broadcast_in_dim.62), kind=kLoop, calls=%fused_computation.41 | loop fusion | flops 147456 | bytes 590016 | tf_op jit(solution)/shard_map/transpose | solution.py:206
  96.8 1.2 copy-done.2
  98.7 7.7 %fusion.97 = (bf16[4,24,16,8,8]{1,4,3,2,0:T(8,128)(2,1)}, f32[4,24,16,8,8]{1,4,3,2,0:T(8,128)}) fusion(f32[4,24,16,1,8]{1,4,3,2,0:T(8,128)S(1)} %get-tuple-element.26, f32[4,24,16,1,8]{1,4,3,2,0:T(8,128)S(1)} %get-tuple-element.27, f32[4,24,16,8,8]{1,3,2,0,4:T(8,128)S(1)} %pad_add_fusion, f32[4,1,16,8,8]{1,4,3,2,0:T(8,128)S(1)} %bitcast.148, ...), kind=kLoop, calls=%fused_computation.176 | loop fusion | flops 2752512 | bytes 3780800 | tf_op jit(solution)/shard_map/convert_element_type | solution.py:212
  106.3 1.6 %copy.152 = bf16[4,24,8,128]{3,1,0,2:T(8,128)(2,1)S(1)} copy(bf16[4,24,8,128]{1,3,2,0:T(8,128)(2,1)} %bitcast.154) | data formatting | bytes 393216 | tf_op jit(solution)/shard_map/convert_element_type | solution.py:212
  107.9 21.1 %all_to_all.40 = bf16[4,24,8,128]{3,1,0,2:T(8,128)(2,1)S(1)} all-to-all(bf16[4,24,8,128]{3,1,0,2:T(8,128)(2,1)S(1)} %copy.152), channel_id=1, replica_groups=mesh['blk'=64,'spec'=8] {'spec'}, dimensions={2} | all-to-all | bytes 393216 | tf_op jit(solution)/shard_map/all_to_all | solution.py:216
  132.4 0.8 copy.174
  133.3 3.5 %all-to-all-start.3 = ((f32[8,4,24,128]{3,1,2,0:T(4,128)}), f32[8,4,24,128]{3,1,2,0:T(4,128)S(1)}, u32[]{:S(2)}, u32[]{:S(2)}) async-start(f32[8,4,24,128]{3,1,2,0:T(4,128)} %copy.174), calls=%async_computation.3 | async-start | bytes 786432 | tf_op jit(solution)/shard_map/all_to_all | solution.py:223
  137.6 13.1 %all-to-all-done.3 = f32[8,4,24,128]{3,1,2,0:T(4,128)S(1)} async-done(((f32[8,4,24,128]{3,1,2,0:T(4,128)}), f32[8,4,24,128]{3,1,2,0:T(4,128)S(1)}, u32[]{:S(2)}, u32[]{:S(2)}) %all-to-all-start.3) | async-done | bytes 393248 | tf_op jit(solution)/shard_map/all_to_all | solution.py:223
  151.0 0.9 fusion.23
  (122 shorter events, 9.8 us)
Async XLA Ops:
  4.9 49.0 %all-to-all-start = ((s32[64,1,2]{2,1,0:T(1,128)}), s32[64,1,2]{2,1,0:T(1,128)}, u32[]{:S(2)}, u32[]{:S(2)}) async-start(s32[64,1,2]{2,1,0:T(1,128)} %copy.142), calls=%async_computation | async-start | bytes 65536 | tf_op jit(solution)/shard_map/all_to_all | solution.py:199
  15.9 7.0 %copy-start.29 = (f32[4]{0:T(128)}, f32[4]{0:T(128)S(1)}, u32[]{:S(2)}) copy-start(f32[4]{0:T(128)S(1)} %get-tuple-element.41) | copy-start | bytes 52
  16.0 7.0 %copy-start.31 = (f32[4]{0:T(128)}, f32[4]{0:T(128)S(1)}, u32[]{:S(2)}) copy-start(f32[4]{0:T(128)S(1)} %broadcast_multiply_fusion.3) | copy-start | bytes 52
  16.0 12.7 %copy-start.21 = (f32[24]{0:T(128)}, f32[24]{0:T(128)S(1)}, u32[]{:S(2)}) copy-start(f32[24]{0:T(128)S(1)} %get-tuple-element.43) | copy-start | bytes 292
  16.0 12.7 %copy-start.24 = (f32[24]{0:T(128)}, f32[24]{0:T(128)S(1)}, u32[]{:S(2)}) copy-start(f32[24]{0:T(128)S(1)} %get-tuple-element.44) | copy-start | bytes 292
  19.3 3.6 %copy-start.11 = (f32[16,8,8]{2,1,0:T(8,128)}, f32[16,8,8]{2,1,0:T(8,128)S(1)}, u32[]{:S(2)}) copy-start(f32[16,8,8]{2,1,0:T(8,128)S(1)} %add.194) | copy-start | bytes 12292
  19.4 3.5 %copy-start.13 = (f32[16,8,8]{2,1,0:T(8,128)}, f32[16,8,8]{2,1,0:T(8,128)S(1)}, u32[]{:S(2)}) copy-start(f32[16,8,8]{2,1,0:T(8,128)S(1)} %add.197) | copy-start | bytes 12292
  20.3 2.7 %copy-start.15 = (f32[16,8,8]{2,1,0:T(8,128)}, f32[16,8,8]{2,1,0:T(8,128)S(1)}, u32[]{:S(2)}) copy-start(f32[16,8,8]{2,1,0:T(8,128)S(1)} %mul.536) | copy-start | bytes 12292
  23.0 1.4 copy-start
  23.0 2.7 %copy-start.5 = (f32[4,24,16,8,8]{1,4,3,2,0:T(8,128)}, f32[4,24,16,8,8]{1,4,3,2,0:T(8,128)S(1)}, u32[]{:S(2)}) copy-start(f32[4,24,16,8,8]{1,4,3,2,0:T(8,128)S(1)} %get-tuple-element.30) | copy-start | bytes 1179652
  30.0 2.5 %copy-start.8 = (f32[4,24,16,8,1]{1,4,3,2,0:T(1,128)S(1)}, f32[4,24,16,8,1]{1,4,3,2,0:T(1,128)}, u32[]{:S(2)}) copy-start(f32[4,24,16,8,1]{1,4,3,2,0:T(1,128)} %get-tuple-element.20) | copy-start | bytes 147460
  30.0 2.5 %copy-start.9 = (f32[4,24,16,1,8]{1,4,3,2,0:T(8,128)S(1)}, f32[4,24,16,1,8]{1,4,3,2,0:T(8,128)}, u32[]{:S(2)}) copy-start(f32[4,24,16,1,8]{1,4,3,2,0:T(8,128)} %get-tuple-element.21) | copy-start | bytes 147460
  30.0 2.5 %copy-start.10 = (f32[4,24,16,1,8]{1,4,3,2,0:T(8,128)S(1)}, f32[4,24,16,1,8]{1,4,3,2,0:T(8,128)}, u32[]{:S(2)}) copy-start(f32[4,24,16,1,8]{1,4,3,2,0:T(8,128)} %get-tuple-element.22) | copy-start | bytes 147460
  32.4 1.1 copy-start.36
  44.2 3.3 %copy-start.33 = (pred[64]{0:T(512)(128)(4,1)S(1)}, pred[64]{0:T(512)(128)(4,1)}, u32[]{:S(2)}) copy-start(pred[64]{0:T(512)(128)(4,1)} %get-tuple-element.37) | copy-start | bytes 196
  44.2 3.4 %copy-start.35 = (pred[64]{0:T(512)(128)(4,1)S(1)}, pred[64]{0:T(512)(128)(4,1)}, u32[]{:S(2)}) copy-start(pred[64]{0:T(512)(128)(4,1)} %get-tuple-element.13) | copy-start | bytes 196
  48.3 3.7 %copy-start.3 = (f32[4,24,16,8,8]{1,4,3,2,0:T(8,128)S(1)}, f32[4,24,16,8,8]{1,4,3,2,0:T(8,128)}, u32[]{:S(2)}) copy-start(f32[4,24,16,8,8]{1,4,3,2,0:T(8,128)} %get-tuple-element.24) | copy-start | bytes 1179652
  60.0 24.6 %all-to-all-start.1 = ((f32[64,2,768]{2,1,0:T(2,128)}), f32[64,2,768]{2,1,0:T(2,128)}, u32[]{:S(2)}, u32[]{:S(2)}) async-start(f32[64,2,768]{2,1,0:T(2,128)} %broadcast_select_fusion), calls=%async_computation.1 | async-start | bytes 786432 | tf_op jit(solution)/shard_map/all_to_all | solution.py:201
  70.5 4.4 %copy-start.1 = (f32[4,24,16,8,8]{1,4,3,2,0:T(8,128)S(1)}, f32[4,24,16,8,8]{1,4,3,2,0:T(8,128)}, u32[]{:S(2)}) copy-start(f32[4,24,16,8,8]{1,4,3,2,0:T(8,128)} %copy-done) | copy-start | bytes 1179652
  91.2 3.2 %copy-start.28 = (pred[16,4]{1,0:T(8,128)(4,1)S(1)}, pred[16,4]{1,0:T(8,128)(4,1)}, u32[]{:S(2)}) copy-start(pred[16,4]{1,0:T(8,128)(4,1)} %broadcast_in_dim.69) | copy-start | bytes 196
  94.3 2.4 %copy-start.6 = (f32[4,1,16,8,8]{1,4,3,2,0:T(8,128)S(1)}, f32[4,1,16,8,8]{1,4,3,2,0:T(8,128)}, u32[]{:S(2)}) copy-start(f32[4,1,16,8,8]{1,4,3,2,0:T(8,128)} %slice.162) | copy-start | bytes 49156
  96.4 1.6 %copy-start.2 = (f32[4,24,16,8,8]{1,4,3,2,0:T(8,128)S(1)}, f32[4,24,16,8,8]{1,4,3,2,0:T(8,128)}, u32[]{:S(2)}) copy-start(f32[4,24,16,8,8]{1,4,3,2,0:T(8,128)} %get-tuple-element.23) | copy-start | bytes 1179652
  96.4 2.3 %copy-start.4 = (f32[4,24,16,8,8]{1,4,3,2,0:T(8,128)S(1)}, f32[4,24,16,8,8]{1,4,3,2,0:T(8,128)}, u32[]{:S(2)}) copy-start(f32[4,24,16,8,8]{1,4,3,2,0:T(8,128)} %get-tuple-element.24) | copy-start | bytes 1179652
  96.4 2.3 %copy-start.12 = (f32[16,8,8]{2,1,0:T(8,128)S(1)}, f32[16,8,8]{2,1,0:T(8,128)}, u32[]{:S(2)}) copy-start(f32[16,8,8]{2,1,0:T(8,128)} %copy-done.11) | copy-start | bytes 12292
  96.4 2.2 %copy-start.14 = (f32[16,8,8]{2,1,0:T(8,128)S(1)}, f32[16,8,8]{2,1,0:T(8,128)}, u32[]{:S(2)}) copy-start(f32[16,8,8]{2,1,0:T(8,128)} %copy-done.13) | copy-start | bytes 12292
  96.4 2.2 %copy-start.16 = (f32[16,8,8]{2,1,0:T(8,128)S(1)}, f32[16,8,8]{2,1,0:T(8,128)}, u32[]{:S(2)}) copy-start(f32[16,8,8]{2,1,0:T(8,128)} %copy-done.15) | copy-start | bytes 12292
  96.4 2.2 %copy-start.22 = (f32[24]{0:T(128)S(1)}, f32[24]{0:T(128)}, u32[]{:S(2)}) copy-start(f32[24]{0:T(128)} %copy-done.21) | copy-start | bytes 292
  96.4 2.2 %copy-start.25 = (f32[24]{0:T(128)S(1)}, f32[24]{0:T(128)}, u32[]{:S(2)}) copy-start(f32[24]{0:T(128)} %copy-done.24) | copy-start | bytes 292
  98.6 30.5 %copy-start.18 = (bf16[2,32,32]{2,1,0:T(8,128)(2,1)S(1)}, bf16[2,32,32]{2,1,0:T(8,128)(2,1)}, u32[]{:S(2)}) copy-start(bf16[2,32,32]{2,1,0:T(8,128)(2,1)} %param.19) | copy-start | bytes 12292
  106.3 23.0 %copy-start.17 = (bf16[2,2,24,24]{3,2,1,0:T(8,128)(2,1)S(1)}, bf16[2,2,24,24]{3,2,1,0:T(8,128)(2,1)}, u32[]{:S(2)}) copy-start(bf16[2,2,24,24]{3,2,1,0:T(8,128)(2,1)} %param.20) | copy-start | bytes 13828
  107.9 22.4 %copy-start.34 = (f32[32]{0:T(128)S(1)}, f32[32]{0:T(128)}, u32[]{:S(2)}) copy-start(f32[32]{0:T(128)} %param.21) | copy-start | bytes 388
  131.7 5.1 %copy-start.19 = (s32[1024]{0:T(1024)S(1)}, s32[1024]{0:T(1024)}, u32[]{:S(2)}) copy-start(s32[1024]{0:T(1024)} %param.16) | copy-start | bytes 12292
  131.7 5.1 %copy-start.27 = (f32[2,1024]{1,0:T(2,128)S(1)}, f32[2,1024]{1,0:T(2,128)}, u32[]{:S(2)}) copy-start(f32[2,1024]{1,0:T(2,128)} %param.15) | copy-start | bytes 24580
  131.7 5.1 %copy-start.20 = (f32[1024]{0:T(1024)S(1)}, f32[1024]{0:T(1024)}, u32[]{:S(2)}) copy-start(f32[1024]{0:T(1024)} %param.12) | copy-start | bytes 12292
  131.7 5.1 %copy-start.30 = (f32[4]{0:T(128)S(1)}, f32[4]{0:T(128)}, u32[]{:S(2)}) copy-start(f32[4]{0:T(128)} %copy-done.29) | copy-start | bytes 52
  131.7 5.1 %copy-start.32 = (f32[4]{0:T(128)S(1)}, f32[4]{0:T(128)}, u32[]{:S(2)}) copy-start(f32[4]{0:T(128)} %copy-done.31) | copy-start | bytes 52
  131.7 5.2 %copy-start.23 = (f32[24]{0:T(128)S(1)}, f32[24]{0:T(128)}, u32[]{:S(2)}) copy-start(f32[24]{0:T(128)} %copy-done.21) | copy-start | bytes 292
  131.7 5.2 %copy-start.26 = (f32[24]{0:T(128)S(1)}, f32[24]{0:T(128)}, u32[]{:S(2)}) copy-start(f32[24]{0:T(128)} %copy-done.24) | copy-start | bytes 292
  131.8 5.3 %copy-start.7 = (f32[4,24,16,8,8]{1,4,3,2,0:T(8,128)S(1)}, f32[4,24,16,8,8]{1,4,3,2,0:T(8,128)}, u32[]{:S(2)}) copy-start(f32[4,24,16,8,8]{1,4,3,2,0:T(8,128)} %get-tuple-element.10) | copy-start | bytes 1179652
  133.3 17.5 %all-to-all-start.3 = ((f32[8,4,24,128]{3,1,2,0:T(4,128)}), f32[8,4,24,128]{3,1,2,0:T(4,128)S(1)}, u32[]{:S(2)}, u32[]{:S(2)}) async-start(f32[8,4,24,128]{3,1,2,0:T(4,128)} %copy.174), calls=%async_computation.3 | async-start | bytes 786432 | tf_op jit(solution)/shard_map/all_to_all | solution.py:223
where the time goes:
time: 153 us; the launch traced here: 152 us
  local copies, waits for them, and re-layouts  47.4 us (31%)
  other arithmetic  34.7 us (23%)
  starting transfers between devices  24.9 us (16%)
  blocking collectives  21.1 us (14%)
  waiting for transfers between devices  20.1 us (13%)
  matrix products  2.79 us (2%)
    all_to_all x1, blocking collectives, shards(): lax.all_to_all(levels, 'spec', split_axis=2, concat_axis=0, tiled=True)  21.1 us
    all_to_all x1, waiting for transfers between devices, shards(): lax.all_to_all(split_rows, 'spec', split_axis=0, concat_axis=0, tiled=True)  13.1 us
    all_to_all x1, starting transfers between devices, shards(): lax.all_to_all(requests, 'blk', split_axis=0, concat_axis=0, tiled=True)  11 us
    all_to_all x1, starting transfers between devices, shards(): lax.all_to_all(located, 'blk', split_axis=0, concat_axis=0, tiled=True)  10.5 us
    gather x3, local copies, waits for them, and re-layouts, shards(): jnp.take(replies.reshape(peer_count * capacity, -1), remote_index, axis=0)  8.47 us
    convert_element_type x1, other arithmetic, shards(): moved.astype(jnp.bfloat16)  7.67 us
    gather x3, local copies, waits for them, and re-layouts, shards(): local_rows = jnp.take(edge_rows, wanted_ids, axis=0)  7.21 us
    all_to_all x1, waiting for transfers between devices, shards(): lax.all_to_all(located, 'blk', split_axis=0, concat_axis=0, tiled=True)  7 us
  transfers between devices with their start and end apart: 3, of which 2 were waited for; matrix products, arithmetic and copies ran while one was open for 29% of the time, Pallas kernels for 0%

commit v1 on v0

v1 whole, which is shorter than its diff:
```python
import math

import jax
import jax.numpy as jnp
from jax import lax
from jax.experimental import pallas as pl
from jax.experimental.pallas import tpu as pltpu
from jax.sharding import PartitionSpec as P

MESH = pl.DeviceIdType.MESH
F32, BF16, I32 = jnp.float32, jnp.bfloat16, jnp.int32

GRAVITY = 9.81
TIME_STEP = 200.0
CELL_SIZE = 5500.0
LOWEST_FREQ = 0.0418
FREQ_GROWTH = 1.1
WIND_GROWTH = 0.0003
TURN_LIMIT = 0.9

FREQS, FL, DIRS, PTS, LANES = 32, 4, 24, 1024, 128
ROWS = FL * DIRS
NB, NZ, NBLK, NFACE = 64, 8, 16, 64
NCH = PTS // LANES
GRP = 8 * DIRS
EDGE_SCALE = 26000.0
CODE_MAX = 32767.0
PEAK_SCALE = 1024.0


def iota(shape, axis):
    return lax.broadcasted_iota(I32, shape, axis)


def dot(a, b):
    return jnp.dot(a, b, preferred_element_type=F32)


def dot_nt(a, b):
    return lax.dot_general(a, b, (((1,), (1,)), ((), ())), preferred_element_type=F32)


def by_direction(x):
    return [x.reshape(FREQS, 3, 8, LANES)[:, t].reshape(FREQS * 8, LANES) for t in range(3)]


def to_freq_form(x):
    return jnp.concatenate(by_direction(x), axis=1)


def from_freq_form(x):
    parts = [x[:, t * LANES:(t + 1) * LANES].reshape(FREQS, 1, 8, LANES) for t in range(3)]
    return jnp.concatenate(parts, axis=1).reshape(FREQS * DIRS, LANES)


def to_angle_form(x):
    return jnp.concatenate([x[g * GRP:(g + 1) * GRP] for g in range(4)], axis=1)


def from_angle_form(x):
    return jnp.concatenate([x[:, g * LANES:(g + 1) * LANES] for g in range(4)], axis=0)


def kernel(
    field_hbm, depth_ref, cur_ref, slope_ref, wind_ref, wet_ref, owner_ref, block_ref, fw_ref, aw_ref, rate_ref,
    out_ref,
    field, mv, g1, wetr, lev, lrecv, pool, trw, trs, reqs, reqr, req_sm, ridx, ridx_sm, esend, erecv,
    tsend, trecv, ssend, srecv, kf, kt, bd, bt, ratew, shoal,
    in_sem, sm_sem, q_send, q_recv, e_send, e_recv, l_send, l_recv, t_send, t_recv, s_send, s_recv,
):
    me = lax.axis_index("blk")
    z = lax.axis_index("spec")
    barrier = pltpu.get_barrier_semaphore()

    load = pltpu.make_async_copy(field_hbm, field, in_sem)
    load.start()

    def greet_blk(j, c):
        pl.semaphore_signal(barrier, inc=1, device_id={"blk": lax.rem(me + j, NB)}, device_id_type=MESH)
        return c

    def greet_spec(j, c):
        pl.semaphore_signal(barrier, inc=1, device_id={"spec": lax.rem(z + j, NZ)}, device_id_type=MESH)
        return c

    lax.fori_loop(1, NB, greet_blk, 0)
    lax.fori_loop(1, NZ, greet_spec, 0)

    own = owner_ref[...]
    ri, ci = iota((NFACE, NFACE), 0), iota((NFACE, NFACE), 1)
    ol = jnp.broadcast_to(own, (NFACE, NFACE))
    os = jnp.sum(jnp.where(ri == ci, ol, 0), axis=1, keepdims=True)
    same = jnp.where(os == ol, 1, 0)
    rank = jnp.sum(jnp.where(ri < ci, same, 0), axis=0, keepdims=True)
    lane = iota((1, NFACE), 1)
    wanted = (block_ref[...] * 4 + jnp.bitwise_xor(jnp.bitwise_and(lane, 3), 1))
    hit = jnp.where(ol == ri, 1, 0)
    first = jnp.where(rank == 0, wanted, 0)
    second = jnp.where(rank == 1, wanted, 0)
    ask0 = jnp.sum(hit * first, axis=1, keepdims=True)
    ask1 = jnp.sum(hit * second, axis=1, keepdims=True)
    li = iota((NFACE, LANES), 1)
    asks = jnp.where(li == 0, ask0, jnp.where(li == 1, ask1, 0))
    for p in range(NB):
        reqs[p] = asks[p:p + 1, :]
    zpad = jnp.zeros((1, LANES - NFACE), I32)
    si = iota((8, LANES), 0)
    wide = [jnp.concatenate([v, zpad], axis=1) for v in (own, jnp.bitwise_and(rank, 1) * 16, wanted)]
    table = jnp.where(si == 0, wide[0], jnp.where(si == 1, wide[1], jnp.where(si == 2, wide[2], 0)))
    ridx[...] = table
    move_idx = pltpu.make_async_copy(ridx, ridx_sm, sm_sem.at[0])
    move_idx.start()

    pl.semaphore_wait(barrier, NB - 1 + NZ - 1)

    def ask(j, c):
        p = lax.rem(me + j, NB)
        pltpu.make_async_remote_copy(
            src_ref=reqs.at[p], dst_ref=reqr.at[me], send_sem=q_send, recv_sem=q_recv,
            device_id={"blk": p}, device_id_type=MESH,
        ).start()
        return c

    lax.fori_loop(1, NB, ask, 0)

    depth = depth_ref[...]
    base_index = (z * FL).astype(F32)
    freqs = []
    for f in range(FL):
        power = jnp.exp((jnp.full((8, LANES), f, F32) + base_index) * math.log(FREQ_GROWTH))
        rf = power * (2.0 * math.pi * LOWEST_FREQ)
        deep = rf * rf / GRAVITY * depth
        kh = deep / jnp.sqrt(jnp.tanh(deep))
        decay = jnp.exp(-2.0 * kh)
        denom = 1.0 - decay * decay
        phase = rf * depth / kh
        shoal[0, f] = 0.5 * (1.0 + 4.0 * kh * decay / denom) * phase
        shoal[1, f] = 2.0 * rf * decay / denom
        shoal[2, f] = 1.0 / phase
        freqs.append(rf[0:1, :])
    angle = iota((DIRS, LANES), 0).astype(F32) * (2.0 * math.pi / DIRS)
    cosine, sine = jnp.cos(angle), jnp.sin(angle)
    grid_ratio = TIME_STEP / CELL_SIZE
    turn_ratio = TIME_STEP / (2.0 * math.pi / DIRS)
    shape = (FL, DIRS, LANES)
    lane3 = iota(shape, 2)
    col = jnp.bitwise_and(lane3, 7)
    row = jnp.bitwise_and(lax.shift_right_logical(lane3, 3), 7)
    rfcol = jnp.concatenate([f.reshape(1, 1, LANES) for f in freqs], axis=0)
    load.wait()
    pad_rows = jnp.zeros((LANES - ROWS, LANES), F32)
    for k in range(NCH):
        sl = slice(k * LANES, (k + 1) * LANES)
        e = field[:, :, sl]
        wet = wet_ref[k:k + 1, :].astype(F32)
        group = shoal[0, :, k:k + 1, :]
        turnf = shoal[1, :, k:k + 1, :]
        slow = shoal[2, :, k:k + 1, :]
        cx = (group * cosine[None] + cur_ref[0:1, sl][None]) * grid_ratio * wet[None]
        cy = (group * sine[None] + cur_ref[1:2, sl][None]) * grid_ratio * wet[None]
        bend = sine * slope_ref[0:1, sl] - cosine * slope_ref[1:2, sl]
        ct = jnp.clip(turnf * bend[None] * turn_ratio, -TURN_LIMIT, TURN_LIMIT)
        right = jnp.maximum(cx, 0.0) * e
        left = jnp.maximum(-cx, 0.0) * e
        up = jnp.maximum(cy, 0.0) * e
        down = jnp.maximum(-cy, 0.0) * e
        ahead = jnp.maximum(ct, 0.0) * e
        back = jnp.maximum(-ct, 0.0) * e
        we = jnp.where(col == 0, left, jnp.where(col == 7, right, 0.0)).reshape(ROWS, LANES)
        sn = jnp.where(row == 0, down, jnp.where(row == 7, up, 0.0)).reshape(ROWS, LANES)
        trw[k, :LANES] = jnp.transpose(jnp.concatenate([we, pad_rows], axis=0))
        trs[k, :LANES] = jnp.transpose(jnp.concatenate([sn, pad_rows], axis=0))
        acc = e - (right + left + up + down + ahead + back)
        acc = acc + jnp.where(col == 0, 0.0, pltpu.roll(right, 1, axis=2))
        acc = acc + jnp.where(col == 7, 0.0, pltpu.roll(left, LANES - 1, axis=2))
        acc = acc + jnp.where(row == 0, 0.0, pltpu.roll(up, 8, axis=2))
        acc = acc + jnp.where(row == 7, 0.0, pltpu.roll(down, LANES - 8, axis=2))
        acc = acc + jnp.concatenate([ahead[:, DIRS - 1:], ahead[:, :DIRS - 1]], axis=1)
        acc = acc + jnp.concatenate([back[:, 1:], back[:, :1]], axis=1)
        mv[k] = acc.reshape(ROWS, LANES)
        along = wind_ref[0:1, sl] * cosine + wind_ref[1:2, sl] * sine
        grow = TIME_STEP * WIND_GROWTH * rfcol * jnp.maximum(along[None] * slow - 1.0, 0.0)
        g1[k] = (wet[None] * (1.0 + grow)).reshape(ROWS, LANES)
        wetr[k] = wet
        for b in range(2):
            base = b * 64
            idx = (2 * k + b) * 4
            pool[idx + 0] = trw[k, pl.ds(base, 8, stride=8), :]
            pool[idx + 1] = trw[k, pl.ds(base + 7, 8, stride=8), :]
            pool[idx + 2] = trs[k, base:base + 8, :]
            pool[idx + 3] = trs[k, base + 56:base + 64, :]

    pltpu.make_async_remote_copy(
        src_ref=reqs.at[pl.ds(0, NB - 1)], dst_ref=reqr.at[pl.ds(0, NB - 1)], send_sem=q_send, recv_sem=q_recv,
        device_id={"blk": me}, device_id_type=MESH,
    ).wait()
    reqr[me] = jnp.zeros((1, LANES), I32)
    move_req = pltpu.make_async_copy(reqr, req_sm, sm_sem.at[1])
    move_req.start()
    move_req.wait()

    def code(x):
        return jnp.minimum(x * EDGE_SCALE + 0.5, 65535.0).astype(I32)

    def pack(j, c):
        p = lax.rem(me + j, NB)
        a = code(pool[req_sm[p, 0, 0]])
        b = code(pool[req_sm[p, 0, 1]])
        esend[p] = jnp.bitwise_or(a, jnp.left_shift(b, 16))
        return c

    def give(j, c):
        p = lax.rem(me + j, NB)
        pltpu.make_async_remote_copy(
            src_ref=esend.at[p], dst_ref=erecv.at[me], send_sem=e_send, recv_sem=e_recv,
            device_id={"blk": p}, device_id_type=MESH,
        ).start()
        return c

    lax.fori_loop(1, NB, pack, 0)
    lax.fori_loop(1, NB, give, 0)

    spread = jnp.where(lax.shift_right_logical(iota((256, FREQS), 0), 3) == iota((256, FREQS), 1), 1.0, 0.0).astype(BF16)
    same_i = jnp.bitwise_and(iota((256, 256), 0), 7) == jnp.bitwise_and(iota((256, 256), 1), 7)
    for s in range(2):
        w = fw_ref[s]
        kf[s] = jnp.where(same_i, dot_nt(dot(spread, w).astype(BF16), spread), 0.0).astype(BF16)
        kt[s] = jnp.where(same_i, dot_nt(dot_nt(spread, w).astype(BF16), spread), 0.0).astype(BF16)

    def over(x):
        return lax.shift_right_logical(x * 2731, 16)

    r24 = iota((GRP, DIRS), 0)
    fan = jnp.where(r24 - DIRS * over(r24) == iota((GRP, DIRS), 1), 1.0, 0.0).astype(BF16)
    same_g = over(iota((GRP, GRP), 0)) == over(iota((GRP, GRP), 1))
    for m in range(2):
        for s in range(2):
            a = aw_ref[m, s]
            bd[m, s] = jnp.where(same_g, dot_nt(dot(fan, a).astype(BF16), fan), 0.0).astype(BF16)
            bt[m, s] = jnp.where(same_g, dot_nt(dot_nt(fan, a).astype(BF16), fan), 0.0).astype(BF16)
    for g in range(4):
        pick = over(iota((GRP, FREQS), 0)) + 8 * g == iota((GRP, FREQS), 1)
        column = jnp.sum(jnp.where(pick, rate_ref[...], 0.0), axis=1, keepdims=True)
        ratew[:, g * LANES:(g + 1) * LANES] = jnp.broadcast_to(column, (GRP, LANES))
    for k in range(NCH):
        trw[k, :LANES] = jnp.zeros((LANES, LANES), F32)
        trs[k, :LANES] = jnp.zeros((LANES, LANES), F32)
    erecv[me] = jnp.zeros((8, LANES), I32)
    move_idx.wait()

    pltpu.make_async_remote_copy(
        src_ref=esend.at[pl.ds(0, NB - 1)], dst_ref=erecv.at[pl.ds(0, NB - 1)], send_sem=e_send, recv_sem=e_recv,
        device_id={"blk": me}, device_id_type=MESH,
    ).wait()

    def face(j):
        owner = ridx_sm[0, j]
        got = jnp.bitwise_and(jnp.right_shift(erecv[owner], ridx_sm[1, j]), 65535)
        return jnp.where(owner != me, got.astype(F32) * (1.0 / EDGE_SCALE), pool[ridx_sm[2, j]])

    def finish(k):
        for b in range(2):
            base, j = b * 64, (2 * k + b) * 4
            trw[k, pl.ds(base, 8, stride=8), :] = face(j)
            trw[k, pl.ds(base + 7, 8, stride=8), :] = face(j + 1)
            trs[k, base:base + 8, :] = face(j + 2)
            trs[k, base + 56:base + 64, :] = face(j + 3)
        moved = mv[k] + jnp.transpose(trw[k, :LANES] + trs[k, :LANES])[:ROWS]
        mv[k] = moved
        return moved.astype(BF16)

    def level_copy(k):
        return pltpu.make_async_remote_copy(
            src_ref=lev.at[k], dst_ref=lrecv.at[z], send_sem=l_send.at[k], recv_sem=l_recv.at[z],
            device_id={"spec": k}, device_id_type=MESH,
        )

    for o in (4, 3, 5, 2, 6, 1, 7):
        k = lax.rem(z + o, NZ)
        lev[k] = finish(k)
        level_copy(k).start()
    lrecv[z] = finish(z)
    for k in range(NCH):
        g1[k] = mv[k] * g1[k]

    for o in range(1, NZ):
        k = lax.rem(z + o, NZ)
        pltpu.make_async_remote_copy(
            src_ref=lev.at[k], dst_ref=lrecv.at[k], send_sem=l_send.at[k], recv_sem=l_recv.at[k],
            device_id={"spec": k}, device_id_type=MESH,
        ).wait()

    levels = lrecv[...].reshape(FREQS * DIRS, LANES).astype(F32)
    level_f = to_freq_form(levels).astype(BF16)
    shifted = [to_angle_form(from_freq_form(dot(kf[s], level_f))).astype(BF16) for s in range(2)]
    level_a = to_angle_form(levels)
    square = level_a * level_a
    total = None
    lows = []
    for m in range(2):
        plus, minus = dot(bd[m, 0], shifted[0]), dot(bd[m, 1], shifted[1])
        delta = ratew[...] * (square * (plus + minus) - 2.0 * level_a * plus * minus)
        lows.append(delta.astype(BF16))
        total = delta if total is None else total + delta
    result = None
    for s in range(2):
        backs = dot(bt[0, s], lows[0]) + dot(bt[1, s], lows[1])
        term = dot(kt[s], to_freq_form(from_angle_form(backs)).astype(BF16))
        result = term if result is None else result + term
    result = from_freq_form(result) - 2.0 * from_angle_form(total)
    mv[...] = result.reshape(NZ, ROWS, LANES)

    def ret_copy(k):
        return pltpu.make_async_remote_copy(
            src_ref=tsend.at[k], dst_ref=trecv.at[z], send_sem=t_send.at[k], recv_sem=t_recv.at[z],
            device_id={"spec": k}, device_id_type=MESH,
        )

    def peak_copy(k):
        return pltpu.make_async_remote_copy(
            src_ref=ssend.at[k], dst_ref=srecv.at[z], send_sem=s_send.at[k], recv_sem=s_recv.at[z],
            device_id={"spec": k}, device_id_type=MESH,
        )

    for o in (4, 3, 5, 2, 6, 1, 7):
        k = lax.rem(z + o, NZ)
        t = mv[k]
        peak = jnp.max(jnp.abs(t), axis=0, keepdims=True)
        unit = (peak * PEAK_SCALE).astype(I32) + 1
        y = t * (CODE_MAX * PEAK_SCALE / unit.astype(F32))
        q = (y + jnp.where(y >= 0.0, 0.5, -0.5)).astype(I32)
        tsend[k] = jnp.bitwise_or(jnp.left_shift(q[:ROWS // 2], 16), jnp.bitwise_and(q[ROWS // 2:], 65535))
        ssend[k] = unit
        ret_copy(k).start()
        peak_copy(k).start()

    def emit(k, t):
        at = pl.ds(pl.multiple_of(k * LANES, LANES), LANES)
        out_ref[:, :, at] = (g1[k] + wetr[k] * t).reshape(FL, DIRS, LANES)

    emit(z, mv[z])
    for o in (1, 7, 2, 6, 3, 5, 4):
        k = lax.rem(z + o, NZ)
        for buf, dst, snd, rcv in ((tsend, trecv, t_send, t_recv), (ssend, srecv, s_send, s_recv)):
            pltpu.make_async_remote_copy(
                src_ref=buf.at[k], dst_ref=dst.at[k], send_sem=snd.at[k], recv_sem=rcv.at[k],
                device_id={"spec": k}, device_id_type=MESH,
            ).wait()
        w = trecv[k]
        scale = srecv[k].astype(F32) * (1.0 / (CODE_MAX * PEAK_SCALE))
        high = jnp.right_shift(w, 16).astype(F32)
        low = jnp.right_shift(jnp.left_shift(w, 16), 16).astype(F32)
        emit(k, jnp.concatenate([high, low], axis=0) * scale)


def shards(
    spectrum, depths, currents, slopes, wind_speed, wet_mask, face_owner, face_block,
    freq_weights, angle_weights, transfer_rate,
):
    vmem = pl.BlockSpec(memory_space=pltpu.VMEM)
    dma = pltpu.SemaphoreType.DMA
    return pl.pallas_call(
        kernel,
        out_shape=jax.ShapeDtypeStruct((FL, DIRS, PTS), F32),
        in_specs=[pl.BlockSpec(memory_space=pl.ANY)] + [vmem] * 10,
        out_specs=vmem,
        scratch_shapes=[
            pltpu.VMEM((FL, DIRS, PTS), F32),
            pltpu.VMEM((NCH, ROWS, LANES), F32),
            pltpu.VMEM((NCH, ROWS, LANES), F32),
            pltpu.VMEM((NCH, 1, LANES), F32),
            pltpu.VMEM((NCH, ROWS, LANES), BF16),
            pltpu.VMEM((NCH, ROWS, LANES), BF16),
            pltpu.VMEM((NFACE, 8, LANES), F32),
            pltpu.VMEM((NCH, LANES + 8, LANES), F32),
            pltpu.VMEM((NCH, LANES + 8, LANES), F32),
            pltpu.VMEM((NB, 1, LANES), I32),
            pltpu.VMEM((NB, 1, LANES), I32),
            pltpu.SMEM((NB, 1, LANES), I32),
            pltpu.VMEM((8, LANES), I32),
            pltpu.SMEM((8, LANES), I32),
            pltpu.VMEM((NB, 8, LANES), I32),
            pltpu.VMEM((NB, 8, LANES), I32),
            pltpu.VMEM((NZ, ROWS // 2, LANES), I32),
            pltpu.VMEM((NZ, ROWS // 2, LANES), I32),
            pltpu.VMEM((NZ, 1, LANES), I32),
            pltpu.VMEM((NZ, 1, LANES), I32),
            pltpu.VMEM((2, 256, 256), BF16),
            pltpu.VMEM((2, 256, 256), BF16),
            pltpu.VMEM((2, 2, GRP, GRP), BF16),
            pltpu.VMEM((2, 2, GRP, GRP), BF16),
            pltpu.VMEM((GRP, 4 * LANES), F32),
            pltpu.VMEM((3, FL, 8, LANES), F32),
            dma, dma((2,)), dma, dma, dma, dma,
            dma((NZ,)), dma((NZ,)), dma((NZ,)), dma((NZ,)), dma((NZ,)), dma((NZ,)),
        ],
        compiler_params=pltpu.CompilerParams(collective_id=0, has_side_effects=True),
    )(
        spectrum, depths.reshape(8, LANES), currents, slopes, wind_speed, wet_mask.reshape(8, LANES),
        face_owner.reshape(1, NFACE), face_block.reshape(1, NFACE), freq_weights, angle_weights,
        transfer_rate.reshape(1, FREQS),
    )


def solution(mesh):
    in_specs = (
        P("spec", None, "blk"), P("blk"), P(None, "blk"), P(None, "blk"), P(None, "blk"), P("blk"),
        P("blk", None), P("blk"), P(), P(), P(),
    )
    return jax.shard_map(
        shards, mesh=mesh, in_specs=in_specs, out_specs=P("spec", None, "blk"), check_vma=False
    )
```

time: 153 us -> 52.1 us (0.34)
  the two profiles are of different devices: /device:TPU:6 before, /device:TPU:1 now
where the time goes in v1:
time: 52.1 us; the launch traced here: 51.9 us
  Pallas kernels  50.1 us (96%)
  local copies, waits for them, and re-layouts  1.77 us (3%)
    pallas_call x1, Pallas kernels, shards(): pl.pallas_call(kernel, out_shape=jax.ShapeDtypeStruct((FL, DIRS, PTS), F3...  50.1 us
    unnamed x1, local copies, waits for them, and re-layouts  1.77 us

profile of v1, /device:TPU:1, one launch (start us, length us, event | category | flops | bytes accessed | tf_op | source)
XLA Modules:
  0.0 51.9 jit_solution(7041492348558490871)
XLA Ops:
  0.0 50.1 %shard_map.109 = f32[4,24,1024]{2,1,0:T(8,128)} custom-call(f32[4,24,1024]{2,1,0:T(8,128)} %field_hbm.1, f32[8,128]{1,0:T(8,128)} %bitcast.5, f32[2,1024]{1,0:T(2,128)} %cur_ref.1, f32[2,1024]{1,0:T(2,128)} %slope_ref.1, f32[2,1024]{1,0:T(2,128)} %wind_ref.1, s32[8,128]{1,0:T(8,128)} %bitcast.6, s32[1,64]{1,0:T(1,128)} %bitcast.7, s32[1,64]{1,0:T(1,128)} %bitcast.8, ...), custom_call_target="tpu_custom_call" | custom-call | tf_op jit(solution)/shard_map/pallas_call | solution.py:362
  50.1 1.8 %copy.13 = f32[4,24,1024]{2,1,0:T(8,128)} copy(f32[4,24,1024]{2,1,0:T(8,128)} %shard_map.109) | data formatting | bytes 786432

commit v2 on v1

--- a/solution.py
+++ b/solution.py
@@ -8,6 +8,7 @@
 from jax.sharding import PartitionSpec as P
 
 MESH = pl.DeviceIdType.MESH
+FAR = (4, 3, 5, 2, 6, 1, 7, 0)
 F32, BF16, I32 = jnp.float32, jnp.bfloat16, jnp.int32
 
 GRAVITY = 9.81
@@ -21,6 +22,7 @@
 FREQS, FL, DIRS, PTS, LANES = 32, 4, 24, 1024, 128
 ROWS = FL * DIRS
 NB, NZ, NBLK, NFACE = 64, 8, 16, 64
+LAG = 4
 NCH = PTS // LANES
 GRP = 8 * DIRS
 EDGE_SCALE = 26000.0
@@ -64,9 +66,9 @@
 def kernel(
     field_hbm, depth_ref, cur_ref, slope_ref, wind_ref, wet_ref, owner_ref, block_ref, fw_ref, aw_ref, rate_ref,
     out_ref,
-    field, mv, g1, wetr, lev, lrecv, pool, trw, trs, reqs, reqr, req_sm, ridx, ridx_sm, esend, erecv,
+    field, mv, g1, wetr, lev, lrecv, pool, trw, trs, reqs, line_in, mid, plane_in, table, table_sm, ridx, ridx_sm, esend, erecv,
     tsend, trecv, ssend, srecv, kf, kt, bd, bt, ratew, shoal,
-    in_sem, sm_sem, q_send, q_recv, e_send, e_recv, l_send, l_recv, t_send, t_recv, s_send, s_recv,
+    in_sem, sm_sem, q_send, q_recv, r_send, r_recv, e_send, e_recv, l_send, l_recv, t_send, t_recv, s_send, s_recv,
 ):
     me = lax.axis_index("blk")
     z = lax.axis_index("spec")
@@ -75,16 +77,18 @@
     load = pltpu.make_async_copy(field_hbm, field, in_sem)
     load.start()
 
-    def greet_blk(j, c):
-        pl.semaphore_signal(barrier, inc=1, device_id={"blk": lax.rem(me + j, NB)}, device_id_type=MESH)
-        return c
-
-    def greet_spec(j, c):
-        pl.semaphore_signal(barrier, inc=1, device_id={"spec": lax.rem(z + j, NZ)}, device_id_type=MESH)
-        return c
-
-    lax.fori_loop(1, NB, greet_blk, 0)
-    lax.fori_loop(1, NZ, greet_spec, 0)
+    x, y, c = me // 16, lax.rem(me // 2, 8), lax.rem(me, 2)
+    q = x * 2 + c
+    xs = [lax.rem(x + d, 4) * 16 for d in range(4)]
+    ys = [lax.rem(y + d, 8) * 2 for d in range(8)]
+    cs = [lax.rem(c + d, 2) for d in range(2)]
+    plane = [(dx, dc) for dx in (2, 1, 3, 0) for dc in (1, 0) if dx or dc]
+
+    for d in FAR[:-1]:
+        for at in ({"blk": xs[0] + ys[d] + cs[0]}, {"spec": lax.rem(z + d, NZ)}):
+            pl.semaphore_signal(barrier, inc=1, device_id=at, device_id_type=MESH)
+    for dx, dc in plane:
+        pl.semaphore_signal(barrier, inc=1, device_id={"blk": xs[dx] + ys[0] + cs[dc]}, device_id_type=MESH)
 
     own = owner_ref[...]
     ri, ci = iota((NFACE, NFACE), 0), iota((NFACE, NFACE), 1)
@@ -94,34 +98,31 @@
     rank = jnp.sum(jnp.where(ri < ci, same, 0), axis=0, keepdims=True)
     lane = iota((1, NFACE), 1)
     wanted = (block_ref[...] * 4 + jnp.bitwise_xor(jnp.bitwise_and(lane, 3), 1))
-    hit = jnp.where(ol == ri, 1, 0)
+    peer = jnp.bitwise_and(ri >> 1, 3) * 16 + (ri >> 3) * 2 + jnp.bitwise_and(ri, 1)
+    hit = jnp.where(ol == peer, 1, 0)
     first = jnp.where(rank == 0, wanted, 0)
     second = jnp.where(rank == 1, wanted, 0)
     ask0 = jnp.sum(hit * first, axis=1, keepdims=True)
     ask1 = jnp.sum(hit * second, axis=1, keepdims=True)
-    li = iota((NFACE, LANES), 1)
-    asks = jnp.where(li == 0, ask0, jnp.where(li == 1, ask1, 0))
-    for p in range(NB):
-        reqs[p] = asks[p:p + 1, :]
+    asks = jnp.where(iota((NFACE, LANES), 1) == me, ask0 + 64 * ask1, 0)
+    for d in range(8):
+        reqs[d] = asks[8 * d:8 * d + 8]
     zpad = jnp.zeros((1, LANES - NFACE), I32)
     si = iota((8, LANES), 0)
     wide = [jnp.concatenate([v, zpad], axis=1) for v in (own, jnp.bitwise_and(rank, 1) * 16, wanted)]
-    table = jnp.where(si == 0, wide[0], jnp.where(si == 1, wide[1], jnp.where(si == 2, wide[2], 0)))
-    ridx[...] = table
+    faces = jnp.where(si == 0, wide[0], jnp.where(si == 1, wide[1], jnp.where(si == 2, wide[2], 0)))
+    ridx[...] = faces
     move_idx = pltpu.make_async_copy(ridx, ridx_sm, sm_sem.at[0])
     move_idx.start()
 
-    pl.semaphore_wait(barrier, NB - 1 + NZ - 1)
-
-    def ask(j, c):
-        p = lax.rem(me + j, NB)
+    pl.semaphore_wait(barrier, 21)
+
+    for d in FAR[:-1]:
         pltpu.make_async_remote_copy(
-            src_ref=reqs.at[p], dst_ref=reqr.at[me], send_sem=q_send, recv_sem=q_recv,
-            device_id={"blk": p}, device_id_type=MESH,
+            src_ref=reqs.at[lax.rem(y + d, 8)], dst_ref=line_in.at[y], send_sem=q_send, recv_sem=q_recv,
+            device_id={"blk": xs[0] + ys[d] + cs[0]}, device_id_type=MESH,
         ).start()
-        return c
-
-    lax.fori_loop(1, NB, ask, 0)
+    line_in[y] = reqs[y]
 
     depth = depth_ref[...]
     base_index = (z * FL).astype(F32)
@@ -191,34 +192,49 @@
             pool[idx + 3] = trs[k, base + 56:base + 64, :]
 
     pltpu.make_async_remote_copy(
-        src_ref=reqs.at[pl.ds(0, NB - 1)], dst_ref=reqr.at[pl.ds(0, NB - 1)], send_sem=q_send, recv_sem=q_recv,
+        src_ref=reqs.at[pl.ds(0, 7)], dst_ref=line_in.at[pl.ds(0, 7)], send_sem=q_send, recv_sem=q_recv,
         device_id={"blk": me}, device_id_type=MESH,
     ).wait()
-    reqr[me] = jnp.zeros((1, LANES), I32)
-    move_req = pltpu.make_async_copy(reqr, req_sm, sm_sem.at[1])
+    gathered = jnp.sum(line_in[...], axis=0)
+    for d in range(8):
+        mid[d] = gathered[d:d + 1]
+    for dx, dc in plane:
+        pltpu.make_async_remote_copy(
+            src_ref=mid.at[lax.rem(x + dx, 4) * 2 + cs[dc]], dst_ref=plane_in.at[q], send_sem=r_send, recv_sem=r_recv,
+            device_id={"blk": xs[dx] + ys[0] + cs[dc]}, device_id_type=MESH,
+        ).start()
+    plane_in[q] = mid[q]
+    pltpu.make_async_remote_copy(
+        src_ref=mid.at[pl.ds(0, 7)], dst_ref=plane_in.at[pl.ds(0, 7)], send_sem=r_send, recv_sem=r_recv,
+        device_id={"blk": me}, device_id_type=MESH,
+    ).wait()
+    table[...] = jnp.sum(plane_in[...], axis=0)
+    move_req = pltpu.make_async_copy(table, table_sm, sm_sem.at[1])
     move_req.start()
     move_req.wait()
 
-    def code(x):
-        return jnp.minimum(x * EDGE_SCALE + 0.5, 65535.0).astype(I32)
-
-    def pack(j, c):
-        p = lax.rem(me + j, NB)
-        a = code(pool[req_sm[p, 0, 0]])
-        b = code(pool[req_sm[p, 0, 1]])
-        esend[p] = jnp.bitwise_or(a, jnp.left_shift(b, 16))
-        return c
-
-    def give(j, c):
-        p = lax.rem(me + j, NB)
+    def code(v):
+        return jnp.minimum(v * EDGE_SCALE + 0.5, 65535.0).astype(I32)
+
+    def give(step, p):
         pltpu.make_async_remote_copy(
-            src_ref=esend.at[p], dst_ref=erecv.at[me], send_sem=e_send, recv_sem=e_recv,
+            src_ref=esend.at[step], dst_ref=erecv.at[me], send_sem=e_send, recv_sem=e_recv,
             device_id={"blk": p}, device_id_type=MESH,
         ).start()
-        return c
-
-    lax.fori_loop(1, NB, pack, 0)
-    lax.fori_loop(1, NB, give, 0)
+
+    order = [(dx, dy, dc) for dc in (1, 0) for dx in (2, 1, 3, 0) for dy in FAR if dx or dy or dc]
+    ready = []
+    for step, (dx, dy, dc) in enumerate(order):
+        p = xs[dx] + ys[dy] + cs[dc]
+        ids = table_sm[0, p]
+        a = code(pool[jnp.bitwise_and(ids, 63)])
+        b = code(pool[jnp.bitwise_and(jnp.right_shift(ids, 6), 63)])
+        esend[step] = jnp.bitwise_or(a, jnp.left_shift(b, 16))
+        ready.append((step, p))
+        if len(ready) > LAG:
+            give(*ready.pop(0))
+    for item in ready:
+        give(*item)
 
     spread = jnp.where(lax.shift_right_logical(iota((256, FREQS), 0), 3) == iota((256, FREQS), 1), 1.0, 0.0).astype(BF16)
     same_i = jnp.bitwise_and(iota((256, 256), 0), 7) == jnp.bitwise_and(iota((256, 256), 1), 7)
@@ -275,10 +291,14 @@
             device_id={"spec": k}, device_id_type=MESH,
         )
 
-    for o in (4, 3, 5, 2, 6, 1, 7):
+    previous = None
+    for o in FAR[:-1]:
         k = lax.rem(z + o, NZ)
         lev[k] = finish(k)
-        level_copy(k).start()
+        if previous is not None:
+            level_copy(previous).start()
+        previous = k
+    level_copy(previous).start()
     lrecv[z] = finish(z)
     for k in range(NCH):
         g1[k] = mv[k] * g1[k]
@@ -361,7 +381,7 @@
     dma = pltpu.SemaphoreType.DMA
     return pl.pallas_call(
         kernel,
-        out_shape=jax.ShapeDtypeStruct((FL, DIRS, PTS), F32),
+        out_shape=pltpu.VMEM((FL, DIRS, PTS), F32),
         in_specs=[pl.BlockSpec(memory_space=pl.ANY)] + [vmem] * 10,
         out_specs=vmem,
         scratch_shapes=[
@@ -374,9 +394,12 @@
             pltpu.VMEM((NFACE, 8, LANES), F32),
             pltpu.VMEM((NCH, LANES + 8, LANES), F32),
             pltpu.VMEM((NCH, LANES + 8, LANES), F32),
-            pltpu.VMEM((NB, 1, LANES), I32),
-            pltpu.VMEM((NB, 1, LANES), I32),
-            pltpu.SMEM((NB, 1, LANES), I32),
+            pltpu.VMEM((8, 8, LANES), I32),
+            pltpu.VMEM((8, 8, LANES), I32),
+            pltpu.VMEM((8, 1, LANES), I32),
+            pltpu.VMEM((8, 1, LANES), I32),
+            pltpu.VMEM((1, LANES), I32),
+            pltpu.SMEM((1, LANES), I32),
             pltpu.VMEM((8, LANES), I32),
             pltpu.SMEM((8, LANES), I32),
             pltpu.VMEM((NB, 8, LANES), I32),
@@ -391,7 +414,7 @@
             pltpu.VMEM((2, 2, GRP, GRP), BF16),
             pltpu.VMEM((GRP, 4 * LANES), F32),
             pltpu.VMEM((3, FL, 8, LANES), F32),
-            dma, dma((2,)), dma, dma, dma, dma,
+            dma, dma((2,)), dma, dma, dma, dma, dma, dma,
             dma((NZ,)), dma((NZ,)), dma((NZ,)), dma((NZ,)), dma((NZ,)), dma((NZ,)),
         ],
         compiler_params=pltpu.CompilerParams(collective_id=0, has_side_effects=True),

time: 52.1 us -> 47 us (0.902)
  the two profiles are of different devices: /device:TPU:1 before, /device:TPU:8 now
where the time goes in v2:
time: 47 us; the launch traced here: 46.8 us
  Pallas kernels  46 us (98%)
  local copies, waits for them, and re-layouts  0.75 us (2%)
    pallas_call x1, Pallas kernels, shards(): pl.pallas_call(kernel, out_shape=pltpu.VMEM((FL, DIRS, PTS), F32), in_spe...  46 us

profile of v2, /device:TPU:8, one launch (start us, length us, event | category | flops | bytes accessed | tf_op | source)
XLA Modules:
  0.0 46.8 jit_solution(6359616526448758996)
XLA Ops:
  0.0 46.0 %shard_map.109 = f32[4,24,1024]{2,1,0:T(8,128)S(1)} custom-call(f32[4,24,1024]{2,1,0:T(8,128)} %field_hbm.1, f32[8,128]{1,0:T(8,128)} %bitcast.5, f32[2,1024]{1,0:T(2,128)} %cur_ref.1, f32[2,1024]{1,0:T(2,128)} %slope_ref.1, f32[2,1024]{1,0:T(2,128)} %wind_ref.1, s32[8,128]{1,0:T(8,128)} %bitcast.6, s32[1,64]{1,0:T(1,128)} %bitcast.7, s32[1,64]{1,0:T(1,128)} %bitcast.8, ...), custom_call_target="tpu_custom_call" | custom-call | tf_op jit(solution)/shard_map/pallas_call | solution.py:382
  46.0 0.7 %copy.13 = f32[4,24,1024]{2,1,0:T(8,128)} copy(f32[4,24,1024]{2,1,0:T(8,128)S(1)} %shard_map.109) | data formatting | bytes 786432

commit v3 on v2

--- a/solution.py
+++ b/solution.py
@@ -66,7 +66,7 @@
 def kernel(
     field_hbm, depth_ref, cur_ref, slope_ref, wind_ref, wet_ref, owner_ref, block_ref, fw_ref, aw_ref, rate_ref,
     out_ref,
-    field, mv, g1, wetr, lev, lrecv, pool, trw, trs, reqs, line_in, mid, plane_in, table, table_sm, ridx, ridx_sm, esend, erecv,
+    field, mv, g1, wetr, lev, lrecv, tab, tab_hi, trw, trs, inw, ins, reqs, line_in, mid, plane_in, asked, ridx, ridx_sm, esend, pool,
     tsend, trecv, ssend, srecv, kf, kt, bd, bt, ratew, shoal,
     in_sem, sm_sem, q_send, q_recv, r_send, r_recv, e_send, e_recv, l_send, l_recv, t_send, t_recv, s_send, s_recv,
 ):
@@ -109,8 +109,11 @@
         reqs[d] = asks[8 * d:8 * d + 8]
     zpad = jnp.zeros((1, LANES - NFACE), I32)
     si = iota((8, LANES), 0)
-    wide = [jnp.concatenate([v, zpad], axis=1) for v in (own, jnp.bitwise_and(rank, 1) * 16, wanted)]
-    faces = jnp.where(si == 0, wide[0], jnp.where(si == 1, wide[1], jnp.where(si == 2, wide[2], 0)))
+    here = own == me
+    turn = jnp.where(here, 0, jnp.bitwise_and(rank, 1) * 64)
+    turn = jnp.where(lane < 32, turn, 64 - turn)
+    wide = [jnp.concatenate([v, zpad], axis=1) for v in (jnp.where(here, NB + wanted, own), turn)]
+    faces = jnp.where(si == 0, wide[0], jnp.where(si == 1, wide[1], 0))
     ridx[...] = faces
     move_idx = pltpu.make_async_copy(ridx, ridx_sm, sm_sem.at[0])
     move_idx.start()
@@ -149,8 +152,21 @@
     row = jnp.bitwise_and(lax.shift_right_logical(lane3, 3), 7)
     rfcol = jnp.concatenate([f.reshape(1, 1, LANES) for f in freqs], axis=0)
     load.wait()
-    pad_rows = jnp.zeros((LANES - ROWS, LANES), F32)
-    for k in range(NCH):
+    lane2 = iota((8, LANES), 1)
+
+    def fold(v, step):
+        codes = jnp.minimum(v * EDGE_SCALE + 0.5, 65535.0).astype(I32)
+        words = jnp.bitwise_or(codes[:48], jnp.left_shift(codes[48:], 16))
+        cell = jnp.bitwise_and(iota((16, LANES), 1), 7) if step == 1 else jnp.bitwise_and(lax.shift_right_logical(iota((16, LANES), 1), 3), 7)
+        tail = [pltpu.roll(words[16 * g:16 * g + 16], LANES - step * (6 - 2 * g), axis=1) for g in range(3)]
+        tail = jnp.where(cell < 2, tail[0], jnp.where(cell < 4, tail[1], tail[2]))
+        return jnp.concatenate([words, tail], axis=0)
+
+    for i in range(4):
+        inw[i, :LANES] = jnp.zeros((LANES, LANES), I32)
+        ins[i, :LANES] = jnp.zeros((LANES, LANES), I32)
+    folded = {}
+    for k in (0, 4, 1, 5, 2, 6, 3, 7):
         sl = slice(k * LANES, (k + 1) * LANES)
         e = field[:, :, sl]
         wet = wet_ref[k:k + 1, :].astype(F32)
@@ -169,8 +185,7 @@
         back = jnp.maximum(-ct, 0.0) * e
         we = jnp.where(col == 0, left, jnp.where(col == 7, right, 0.0)).reshape(ROWS, LANES)
         sn = jnp.where(row == 0, down, jnp.where(row == 7, up, 0.0)).reshape(ROWS, LANES)
-        trw[k, :LANES] = jnp.transpose(jnp.concatenate([we, pad_rows], axis=0))
-        trs[k, :LANES] = jnp.transpose(jnp.concatenate([sn, pad_rows], axis=0))
+        folded[k] = fold(we, 8), fold(sn, 1)
         acc = e - (right + left + up + down + ahead + back)
         acc = acc + jnp.where(col == 0, 0.0, pltpu.roll(right, 1, axis=2))
         acc = acc + jnp.where(col == 7, 0.0, pltpu.roll(left, LANES - 1, axis=2))
@@ -183,13 +198,9 @@
         grow = TIME_STEP * WIND_GROWTH * rfcol * jnp.maximum(along[None] * slow - 1.0, 0.0)
         g1[k] = (wet[None] * (1.0 + grow)).reshape(ROWS, LANES)
         wetr[k] = wet
-        for b in range(2):
-            base = b * 64
-            idx = (2 * k + b) * 4
-            pool[idx + 0] = trw[k, pl.ds(base, 8, stride=8), :]
-            pool[idx + 1] = trw[k, pl.ds(base + 7, 8, stride=8), :]
-            pool[idx + 2] = trs[k, base:base + 8, :]
-            pool[idx + 3] = trs[k, base + 56:base + 64, :]
+        if k >= 4:
+            trw[k - 4, :LANES] = jnp.transpose(jnp.concatenate([folded[k - 4][0], folded[k][0]], axis=0))
+            trs[k - 4, :LANES] = jnp.transpose(jnp.concatenate([folded[k - 4][1], folded[k][1]], axis=0))
 
     pltpu.make_async_remote_copy(
         src_ref=reqs.at[pl.ds(0, 7)], dst_ref=line_in.at[pl.ds(0, 7)], send_sem=q_send, recv_sem=q_recv,
@@ -204,21 +215,32 @@
             device_id={"blk": xs[dx] + ys[0] + cs[dc]}, device_id_type=MESH,
         ).start()
     plane_in[q] = mid[q]
+    for k in range(4):
+        for b in range(2):
+            base = b * 64
+            edges = (
+                trw[k, pl.ds(base, 8, stride=8), :], trw[k, pl.ds(base + 7, 8, stride=8), :],
+                trs[k, base:base + 8, :], trs[k, base + 56:base + 64, :],
+            )
+            for side, v in enumerate(edges):
+                at = (2 * k + b) * 4 + side
+                r = pltpu.roll(v, 64, axis=1)
+                for i, (a, o) in ((at, (v, r)), (at + 32, (r, v))):
+                    low = jnp.where(lane2 < 64, a, 0)
+                    tab[i] = low
+                    pool[NB + i] = low
+                    tab_hi[i] = jnp.where(lane2 < 64, 0, o)
     pltpu.make_async_remote_copy(
         src_ref=mid.at[pl.ds(0, 7)], dst_ref=plane_in.at[pl.ds(0, 7)], send_sem=r_send, recv_sem=r_recv,
         device_id={"blk": me}, device_id_type=MESH,
     ).wait()
-    table[...] = jnp.sum(plane_in[...], axis=0)
-    move_req = pltpu.make_async_copy(table, table_sm, sm_sem.at[1])
+    move_req = pltpu.make_async_copy(plane_in, asked, sm_sem.at[1])
     move_req.start()
     move_req.wait()
 
-    def code(v):
-        return jnp.minimum(v * EDGE_SCALE + 0.5, 65535.0).astype(I32)
-
     def give(step, p):
         pltpu.make_async_remote_copy(
-            src_ref=esend.at[step], dst_ref=erecv.at[me], send_sem=e_send, recv_sem=e_recv,
+            src_ref=esend.at[step, pl.ds(0, 6)], dst_ref=pool.at[me, pl.ds(0, 6)], send_sem=e_send, recv_sem=e_recv,
             device_id={"blk": p}, device_id_type=MESH,
         ).start()
 
@@ -226,10 +248,9 @@
     ready = []
     for step, (dx, dy, dc) in enumerate(order):
         p = xs[dx] + ys[dy] + cs[dc]
-        ids = table_sm[0, p]
-        a = code(pool[jnp.bitwise_and(ids, 63)])
-        b = code(pool[jnp.bitwise_and(jnp.right_shift(ids, 6), 63)])
-        esend[step] = jnp.bitwise_or(a, jnp.left_shift(b, 16))
+        ids = asked[lax.rem(x + dx, 4) * 2 + cs[dc], 0, p]
+        low, high = jnp.bitwise_and(ids, 63), jnp.bitwise_and(jnp.right_shift(ids, 6), 63)
+        esend[step] = jnp.bitwise_or(tab[low], tab_hi[high])
         ready.append((step, p))
         if len(ready) > LAG:
             give(*ready.pop(0))
@@ -258,32 +279,50 @@
         pick = over(iota((GRP, FREQS), 0)) + 8 * g == iota((GRP, FREQS), 1)
         column = jnp.sum(jnp.where(pick, rate_ref[...], 0.0), axis=1, keepdims=True)
         ratew[:, g * LANES:(g + 1) * LANES] = jnp.broadcast_to(column, (GRP, LANES))
-    for k in range(NCH):
-        trw[k, :LANES] = jnp.zeros((LANES, LANES), F32)
-        trs[k, :LANES] = jnp.zeros((LANES, LANES), F32)
-    erecv[me] = jnp.zeros((8, LANES), I32)
+    pool[me] = jnp.zeros((8, LANES), I32)
     move_idx.wait()
 
     pltpu.make_async_remote_copy(
-        src_ref=esend.at[pl.ds(0, NB - 1)], dst_ref=erecv.at[pl.ds(0, NB - 1)], send_sem=e_send, recv_sem=e_recv,
+        src_ref=esend.at[pl.ds(0, NB - 1), pl.ds(0, 6)], dst_ref=pool.at[pl.ds(0, NB - 1), pl.ds(0, 6)], send_sem=e_send, recv_sem=e_recv,
         device_id={"blk": me}, device_id_type=MESH,
     ).wait()
 
     def face(j):
-        owner = ridx_sm[0, j]
-        got = jnp.bitwise_and(jnp.right_shift(erecv[owner], ridx_sm[1, j]), 65535)
-        return jnp.where(owner != me, got.astype(F32) * (1.0 / EDGE_SCALE), pool[ridx_sm[2, j]])
-
-    def finish(k):
+        words = pool[ridx_sm[0, j]]
+        return jnp.where(ridx_sm[1, j] > 0, pltpu.roll(words, 64, axis=1), words)
+
+    def both(j):
+        return jnp.where(lane2 < 64, face(j), face(j + 32))
+
+    lane1 = iota((16, LANES), 1)
+    by_row = jnp.bitwise_and(lax.shift_right_logical(lane1, 3), 7) >= 6
+    by_col = jnp.bitwise_and(lane1, 7) >= 6
+
+    def unfold(words, step, mask):
+        tail = words[48:64]
+        parts = [
+            jnp.where(mask, pltpu.roll(tail, step * (6 - 2 * g), axis=1), words[16 * g:16 * g + 16]) for g in range(3)
+        ]
+        return jnp.concatenate(parts, axis=0)
+
+    def finish(slot, m):
         for b in range(2):
-            base, j = b * 64, (2 * k + b) * 4
-            trw[k, pl.ds(base, 8, stride=8), :] = face(j)
-            trw[k, pl.ds(base + 7, 8, stride=8), :] = face(j + 1)
-            trs[k, base:base + 8, :] = face(j + 2)
-            trs[k, base + 56:base + 64, :] = face(j + 3)
-        moved = mv[k] + jnp.transpose(trw[k, :LANES] + trs[k, :LANES])[:ROWS]
-        mv[k] = moved
-        return moved.astype(BF16)
+            base, j = b * 64, (2 * m + b) * 4
+            inw[slot, pl.ds(base, 8, stride=8), :] = both(j)
+            inw[slot, pl.ds(base + 7, 8, stride=8), :] = both(j + 1)
+            ins[slot, base:base + 8, :] = both(j + 2)
+            ins[slot, base + 56:base + 64, :] = both(j + 3)
+        wide_w, wide_s = jnp.transpose(inw[slot, :LANES]), jnp.transpose(ins[slot, :LANES])
+        for h in range(2):
+            k = m + 4 * h
+            west = unfold(wide_w[64 * h:64 * h + 64], 8, by_row)
+            south = unfold(wide_s[64 * h:64 * h + 64], 1, by_col)
+            low = jnp.bitwise_and(west, 65535) + jnp.bitwise_and(south, 65535)
+            high = lax.shift_right_logical(west, 16) + lax.shift_right_logical(south, 16)
+            codes = jnp.concatenate([low, high], axis=0).astype(F32)
+            moved = mv[k] + codes * (1.0 / EDGE_SCALE)
+            mv[k] = moved
+            lev[k] = moved.astype(BF16)
 
     def level_copy(k):
         return pltpu.make_async_remote_copy(
@@ -291,15 +330,16 @@
             device_id={"spec": k}, device_id_type=MESH,
         )
 
-    previous = None
-    for o in FAR[:-1]:
-        k = lax.rem(z + o, NZ)
-        lev[k] = finish(k)
-        if previous is not None:
-            level_copy(previous).start()
-        previous = k
-    level_copy(previous).start()
-    lrecv[z] = finish(z)
+    waiting = ()
+    for slot, (o, nexts) in enumerate(((0, (4,)), (3, (3, 7)), (1, (5, 1)), (2, (2, 6)))):
+        finish(slot, lax.rem(z + o, 4))
+        if slot == 0:
+            lrecv[z] = lev[z]
+        for d in waiting:
+            level_copy(lax.rem(z + d, NZ)).start()
+        waiting = nexts
+    for d in waiting:
+        level_copy(lax.rem(z + d, NZ)).start()
     for k in range(NCH):
         g1[k] = mv[k] * g1[k]
 
@@ -391,19 +431,21 @@
             pltpu.VMEM((NCH, 1, LANES), F32),
             pltpu.VMEM((NCH, ROWS, LANES), BF16),
             pltpu.VMEM((NCH, ROWS, LANES), BF16),
-            pltpu.VMEM((NFACE, 8, LANES), F32),
-            pltpu.VMEM((NCH, LANES + 8, LANES), F32),
-            pltpu.VMEM((NCH, LANES + 8, LANES), F32),
+            pltpu.VMEM((NFACE, 8, LANES), I32),
+            pltpu.VMEM((NFACE, 8, LANES), I32),
+            pltpu.VMEM((4, LANES + 8, LANES), I32),
+            pltpu.VMEM((4, LANES + 8, LANES), I32),
+            pltpu.VMEM((4, LANES + 8, LANES), I32),
+            pltpu.VMEM((4, LANES + 8, LANES), I32),
             pltpu.VMEM((8, 8, LANES), I32),
             pltpu.VMEM((8, 8, LANES), I32),
             pltpu.VMEM((8, 1, LANES), I32),
             pltpu.VMEM((8, 1, LANES), I32),
-            pltpu.VMEM((1, LANES), I32),
-            pltpu.SMEM((1, LANES), I32),
+            pltpu.SMEM((8, 1, LANES), I32),
             pltpu.VMEM((8, LANES), I32),
             pltpu.SMEM((8, LANES), I32),
             pltpu.VMEM((NB, 8, LANES), I32),
-            pltpu.VMEM((NB, 8, LANES), I32),
+            pltpu.VMEM((NB + NFACE, 8, LANES), I32),
             pltpu.VMEM((NZ, ROWS // 2, LANES), I32),
             pltpu.VMEM((NZ, ROWS // 2, LANES), I32),
             pltpu.VMEM((NZ, 1, LANES), I32),

time: 47 us -> 45.7 us (0.972)
  Pallas kernels: 46 us -> 44.8 us
    pallas_call x1, Pallas kernels: 46 us -> 44.8 us  [shards(): pl.pallas_call(kernel, out_shape=pltpu.VMEM((FL, DIRS, PTS), F32), in_spe...]
where the time goes in v3:
time: 45.7 us; the launch traced here: 45.5 us
  Pallas kernels  44.8 us (98%)
  local copies, waits for them, and re-layouts  0.75 us (2%)
    pallas_call x1, Pallas kernels, shards(): pl.pallas_call(kernel, out_shape=pltpu.VMEM((FL, DIRS, PTS), F32), in_spe...  44.8 us

profile of v3, /device:TPU:8, one launch (start us, length us, event | category | flops | bytes accessed | tf_op | source)
XLA Modules:
  0.0 45.5 jit_solution(17786121459609345849)
XLA Ops:
  0.0 44.8 %shard_map.109 = f32[4,24,1024]{2,1,0:T(8,128)S(1)} custom-call(f32[4,24,1024]{2,1,0:T(8,128)} %field_hbm.1, f32[8,128]{1,0:T(8,128)} %bitcast.5, f32[2,1024]{1,0:T(2,128)} %cur_ref.1, f32[2,1024]{1,0:T(2,128)} %slope_ref.1, f32[2,1024]{1,0:T(2,128)} %wind_ref.1, s32[8,128]{1,0:T(8,128)} %bitcast.6, s32[1,64]{1,0:T(1,128)} %bitcast.7, s32[1,64]{1,0:T(1,128)} %bitcast.8, ...), custom_call_target="tpu_custom_call" | custom-call | tf_op jit(solution)/shard_map/pallas_call | solution.py:422
  44.8 0.7 %copy.13 = f32[4,24,1024]{2,1,0:T(8,128)} copy(f32[4,24,1024]{2,1,0:T(8,128)S(1)} %shard_map.109) | data formatting | bytes 786432

commit v4 on v3

--- a/solution.py
+++ b/solution.py
@@ -64,8 +64,9 @@
 
 
 def kernel(
-    field_hbm, depth_ref, cur_ref, slope_ref, wind_ref, wet_ref, owner_ref, block_ref, fw_ref, aw_ref, rate_ref,
+    field_hbm, depth_hbm, cur_hbm, slope_hbm, wind_hbm, wet_hbm, owner_hbm, block_hbm, fw_hbm, aw_hbm, rate_hbm,
     out_ref,
+    depth_ref, cur_ref, slope_ref, wind_ref, wet_ref, owner_ref, block_ref, fw_ref, aw_ref, rate_ref, op_sem,
     field, mv, g1, wetr, lev, lrecv, tab, tab_hi, trw, trs, inw, ins, reqs, line_in, mid, plane_in, asked, ridx, ridx_sm, esend, pool,
     tsend, trecv, ssend, srecv, kf, kt, bd, bt, ratew, shoal,
     in_sem, sm_sem, q_send, q_recv, r_send, r_recv, e_send, e_recv, l_send, l_recv, t_send, t_recv, s_send, s_recv,
@@ -74,9 +75,6 @@
     z = lax.axis_index("spec")
     barrier = pltpu.get_barrier_semaphore()
 
-    load = pltpu.make_async_copy(field_hbm, field, in_sem)
-    load.start()
-
     x, y, c = me // 16, lax.rem(me // 2, 8), lax.rem(me, 2)
     q = x * 2 + c
     xs = [lax.rem(x + d, 4) * 16 for d in range(4)]
@@ -89,6 +87,22 @@
             pl.semaphore_signal(barrier, inc=1, device_id=at, device_id_type=MESH)
     for dx, dc in plane:
         pl.semaphore_signal(barrier, inc=1, device_id={"blk": xs[dx] + ys[0] + cs[dc]}, device_id_type=MESH)
+
+    small = [
+        pltpu.make_async_copy(src, dst, op_sem.at[i]) for i, (src, dst) in enumerate((
+            (owner_hbm, owner_ref), (block_hbm, block_ref), (depth_hbm, depth_ref), (cur_hbm, cur_ref),
+            (slope_hbm, slope_ref), (wind_hbm, wind_ref), (wet_hbm, wet_ref), (fw_hbm, fw_ref), (aw_hbm, aw_ref),
+            (rate_hbm, rate_ref),
+        ))
+    ]
+    for copy in small[:3]:
+        copy.start()
+    load = pltpu.make_async_copy(field_hbm, field, in_sem)
+    load.start()
+    for copy in small[3:]:
+        copy.start()
+    small[0].wait()
+    small[1].wait()
 
     own = owner_ref[...]
     ri, ci = iota((NFACE, NFACE), 0), iota((NFACE, NFACE), 1)
@@ -98,15 +112,14 @@
     rank = jnp.sum(jnp.where(ri < ci, same, 0), axis=0, keepdims=True)
     lane = iota((1, NFACE), 1)
     wanted = (block_ref[...] * 4 + jnp.bitwise_xor(jnp.bitwise_and(lane, 3), 1))
-    peer = jnp.bitwise_and(ri >> 1, 3) * 16 + (ri >> 3) * 2 + jnp.bitwise_and(ri, 1)
-    hit = jnp.where(ol == peer, 1, 0)
-    first = jnp.where(rank == 0, wanted, 0)
-    second = jnp.where(rank == 1, wanted, 0)
-    ask0 = jnp.sum(hit * first, axis=1, keepdims=True)
-    ask1 = jnp.sum(hit * second, axis=1, keepdims=True)
-    asks = jnp.where(iota((NFACE, LANES), 1) == me, ask0 + 64 * ask1, 0)
+    rank_col = jnp.sum(jnp.where(ci < ri, same, 0), axis=1, keepdims=True)
+    wanted_col = jnp.sum(jnp.where(ri == ci, wanted, 0), axis=1, keepdims=True)
+    ask = jnp.where(rank_col == 0, wanted_col, jnp.where(rank_col == 1, wanted_col * 64, 0))
+    li = iota((NFACE, LANES), 1)
+    target = (li >> 5) * 16 + jnp.bitwise_and(li >> 4, 1)
+    ask = jnp.where(jnp.bitwise_and(li, 15) == y, ask, 0)
     for d in range(8):
-        reqs[d] = asks[8 * d:8 * d + 8]
+        reqs[d] = jnp.sum(jnp.where(os == target + 2 * d, ask, 0), axis=0, keepdims=True)
     zpad = jnp.zeros((1, LANES - NFACE), I32)
     si = iota((8, LANES), 0)
     here = own == me
@@ -127,6 +140,7 @@
         ).start()
     line_in[y] = reqs[y]
 
+    small[2].wait()
     depth = depth_ref[...]
     base_index = (z * FL).astype(F32)
     freqs = []
@@ -151,6 +165,8 @@
     col = jnp.bitwise_and(lane3, 7)
     row = jnp.bitwise_and(lax.shift_right_logical(lane3, 3), 7)
     rfcol = jnp.concatenate([f.reshape(1, 1, LANES) for f in freqs], axis=0)
+    for copy in small[3:7]:
+        copy.wait()
     load.wait()
     lane2 = iota((8, LANES), 1)
 
@@ -206,15 +222,13 @@
         src_ref=reqs.at[pl.ds(0, 7)], dst_ref=line_in.at[pl.ds(0, 7)], send_sem=q_send, recv_sem=q_recv,
         device_id={"blk": me}, device_id_type=MESH,
     ).wait()
-    gathered = jnp.sum(line_in[...], axis=0)
-    for d in range(8):
-        mid[d] = gathered[d:d + 1]
+    mid[...] = jnp.sum(line_in[...], axis=0)
     for dx, dc in plane:
         pltpu.make_async_remote_copy(
-            src_ref=mid.at[lax.rem(x + dx, 4) * 2 + cs[dc]], dst_ref=plane_in.at[q], send_sem=r_send, recv_sem=r_recv,
+            src_ref=mid, dst_ref=plane_in.at[q], send_sem=r_send, recv_sem=r_recv,
             device_id={"blk": xs[dx] + ys[0] + cs[dc]}, device_id_type=MESH,
         ).start()
-    plane_in[q] = mid[q]
+    plane_in[q] = mid[...]
     for k in range(4):
         for b in range(2):
             base = b * 64
@@ -231,7 +245,7 @@
                     pool[NB + i] = low
                     tab_hi[i] = jnp.where(lane2 < 64, 0, o)
     pltpu.make_async_remote_copy(
-        src_ref=mid.at[pl.ds(0, 7)], dst_ref=plane_in.at[pl.ds(0, 7)], send_sem=r_send, recv_sem=r_recv,
+        src_ref=plane_in.at[pl.ds(0, 7)], dst_ref=plane_in.at[pl.ds(0, 7)], send_sem=r_send, recv_sem=r_recv,
         device_id={"blk": me}, device_id_type=MESH,
     ).wait()
     move_req = pltpu.make_async_copy(plane_in, asked, sm_sem.at[1])
@@ -248,7 +262,7 @@
     ready = []
     for step, (dx, dy, dc) in enumerate(order):
         p = xs[dx] + ys[dy] + cs[dc]
-        ids = asked[lax.rem(x + dx, 4) * 2 + cs[dc], 0, p]
+        ids = asked[lax.rem(x + dx, 4) * 2 + cs[dc], 0, q * 16 + lax.rem(y + dy, 8)]
         low, high = jnp.bitwise_and(ids, 63), jnp.bitwise_and(jnp.right_shift(ids, 6), 63)
         esend[step] = jnp.bitwise_or(tab[low], tab_hi[high])
         ready.append((step, p))
@@ -257,12 +271,14 @@
     for item in ready:
         give(*item)
 
+    for copy in small[7:]:
+        copy.wait()
     spread = jnp.where(lax.shift_right_logical(iota((256, FREQS), 0), 3) == iota((256, FREQS), 1), 1.0, 0.0).astype(BF16)
     same_i = jnp.bitwise_and(iota((256, 256), 0), 7) == jnp.bitwise_and(iota((256, 256), 1), 7)
     for s in range(2):
         w = fw_ref[s]
-        kf[s] = jnp.where(same_i, dot_nt(dot(spread, w).astype(BF16), spread), 0.0).astype(BF16)
-        kt[s] = jnp.where(same_i, dot_nt(dot_nt(spread, w).astype(BF16), spread), 0.0).astype(BF16)
+        kf[256 * s:256 * s + 256] = jnp.where(same_i, dot_nt(dot(spread, w).astype(BF16), spread), 0.0).astype(BF16)
+        kt[:, 256 * s:256 * s + 256] = jnp.where(same_i, dot_nt(dot_nt(spread, w).astype(BF16), spread), 0.0).astype(BF16)
 
     def over(x):
         return lax.shift_right_logical(x * 2731, 16)
@@ -273,8 +289,8 @@
     for m in range(2):
         for s in range(2):
             a = aw_ref[m, s]
-            bd[m, s] = jnp.where(same_g, dot_nt(dot(fan, a).astype(BF16), fan), 0.0).astype(BF16)
-            bt[m, s] = jnp.where(same_g, dot_nt(dot_nt(fan, a).astype(BF16), fan), 0.0).astype(BF16)
+            bd[s, GRP * m:GRP * m + GRP] = jnp.where(same_g, dot_nt(dot(fan, a).astype(BF16), fan), 0.0).astype(BF16)
+            bt[m, GRP * s:GRP * s + GRP] = jnp.where(same_g, dot_nt(dot_nt(fan, a).astype(BF16), fan), 0.0).astype(BF16)
     for g in range(4):
         pick = over(iota((GRP, FREQS), 0)) + 8 * g == iota((GRP, FREQS), 1)
         column = jnp.sum(jnp.where(pick, rate_ref[...], 0.0), axis=1, keepdims=True)
@@ -352,21 +368,21 @@
 
     levels = lrecv[...].reshape(FREQS * DIRS, LANES).astype(F32)
     level_f = to_freq_form(levels).astype(BF16)
-    shifted = [to_angle_form(from_freq_form(dot(kf[s], level_f))).astype(BF16) for s in range(2)]
+    both_shifted = dot(kf[...], level_f)
+    shifted = [to_angle_form(from_freq_form(both_shifted[256 * s:256 * s + 256])).astype(BF16) for s in range(2)]
     level_a = to_angle_form(levels)
     square = level_a * level_a
+    pluses, minuses = dot(bd[0], shifted[0]), dot(bd[1], shifted[1])
     total = None
     lows = []
     for m in range(2):
-        plus, minus = dot(bd[m, 0], shifted[0]), dot(bd[m, 1], shifted[1])
+        plus, minus = pluses[GRP * m:GRP * m + GRP], minuses[GRP * m:GRP * m + GRP]
         delta = ratew[...] * (square * (plus + minus) - 2.0 * level_a * plus * minus)
         lows.append(delta.astype(BF16))
         total = delta if total is None else total + delta
-    result = None
-    for s in range(2):
-        backs = dot(bt[0, s], lows[0]) + dot(bt[1, s], lows[1])
-        term = dot(kt[s], to_freq_form(from_angle_form(backs)).astype(BF16))
-        result = term if result is None else result + term
+    backs = dot(bt[0], lows[0]) + dot(bt[1], lows[1])
+    backs = [to_freq_form(from_angle_form(backs[GRP * s:GRP * s + GRP])) for s in range(2)]
+    result = dot(kt[...], jnp.concatenate(backs, axis=0).astype(BF16))
     result = from_freq_form(result) - 2.0 * from_angle_form(total)
     mv[...] = result.reshape(NZ, ROWS, LANES)
 
@@ -422,9 +438,12 @@
     return pl.pallas_call(
         kernel,
         out_shape=pltpu.VMEM((FL, DIRS, PTS), F32),
-        in_specs=[pl.BlockSpec(memory_space=pl.ANY)] + [vmem] * 10,
+        in_specs=[pl.BlockSpec(memory_space=pl.ANY)] * 11,
         out_specs=vmem,
         scratch_shapes=[
+            pltpu.VMEM((8, LANES), F32), pltpu.VMEM((2, PTS), F32), pltpu.VMEM((2, PTS), F32), pltpu.VMEM((2, PTS), F32),
+            pltpu.VMEM((8, LANES), I32), pltpu.VMEM((1, NFACE), I32), pltpu.VMEM((1, NFACE), I32),
+            pltpu.VMEM((2, FREQS, FREQS), BF16), pltpu.VMEM((2, 2, DIRS, DIRS), BF16), pltpu.VMEM((1, FREQS), F32), dma((10,)),
             pltpu.VMEM((FL, DIRS, PTS), F32),
             pltpu.VMEM((NCH, ROWS, LANES), F32),
             pltpu.VMEM((NCH, ROWS, LANES), F32),
@@ -437,9 +456,9 @@
             pltpu.VMEM((4, LANES + 8, LANES), I32),
             pltpu.VMEM((4, LANES + 8, LANES), I32),
             pltpu.VMEM((4, LANES + 8, LANES), I32),
-            pltpu.VMEM((8, 8, LANES), I32),
-            pltpu.VMEM((8, 8, LANES), I32),
             pltpu.VMEM((8, 1, LANES), I32),
+            pltpu.VMEM((8, 1, LANES), I32),
+            pltpu.VMEM((1, LANES), I32),
             pltpu.VMEM((8, 1, LANES), I32),
             pltpu.SMEM((8, 1, LANES), I32),
             pltpu.VMEM((8, LANES), I32),
@@ -450,10 +469,10 @@
             pltpu.VMEM((NZ, ROWS // 2, LANES), I32),
             pltpu.VMEM((NZ, 1, LANES), I32),
             pltpu.VMEM((NZ, 1, LANES), I32),
-            pltpu.VMEM((2, 256, 256), BF16),
-            pltpu.VMEM((2, 256, 256), BF16),
-            pltpu.VMEM((2, 2, GRP, GRP), BF16),
-            pltpu.VMEM((2, 2, GRP, GRP), BF16),
+            pltpu.VMEM((512, 256), BF16),
+            pltpu.VMEM((256, 512), BF16),
+            pltpu.VMEM((2, 2 * GRP, GRP), BF16),
+            pltpu.VMEM((2, 2 * GRP, GRP), BF16),
             pltpu.VMEM((GRP, 4 * LANES), F32),
             pltpu.VMEM((3, FL, 8, LANES), F32),
             dma, dma((2,)), dma, dma, dma, dma, dma, dma,

time: 45.7 us -> 44.9 us (0.982)
  Pallas kernels: 44.8 us -> 44 us
    pallas_call x1, Pallas kernels: 44.8 us -> 44 us  [shards(): pl.pallas_call(kernel, out_shape=pltpu.VMEM((FL, DIRS, PTS), F32), in_spe...]
where the time goes in v4:
time: 44.9 us; the launch traced here: 44.8 us
  Pallas kernels  44 us (98%)
  local copies, waits for them, and re-layouts  0.75 us (2%)
    pallas_call x1, Pallas kernels, shards(): pl.pallas_call(kernel, out_shape=pltpu.VMEM((FL, DIRS, PTS), F32), in_spe...  44 us

profile of v4, /device:TPU:8, one launch (start us, length us, event | category | flops | bytes accessed | tf_op | source)
XLA Modules:
  0.0 44.8 jit_solution(303809693605113451)
XLA Ops:
  0.0 44.0 %shard_map.109 = f32[4,24,1024]{2,1,0:T(8,128)S(1)} custom-call(f32[4,24,1024]{2,1,0:T(8,128)} %field_hbm.1, f32[8,128]{1,0:T(8,128)} %bitcast.5, f32[2,1024]{1,0:T(2,128)} %cur_hbm.1, f32[2,1024]{1,0:T(2,128)} %slope_hbm.1, f32[2,1024]{1,0:T(2,128)} %wind_hbm.1, s32[8,128]{1,0:T(8,128)} %bitcast.6, s32[1,64]{1,0:T(1,128)} %bitcast.7, s32[1,64]{1,0:T(1,128)} %bitcast.8, ...), custom_call_target="tpu_custom_call" | custom-call | tf_op jit(solution)/shard_map/pallas_call | solution.py:438
  44.0 0.7 %copy.13 = f32[4,24,1024]{2,1,0:T(8,128)} copy(f32[4,24,1024]{2,1,0:T(8,128)S(1)} %shard_map.109) | data formatting | bytes 786432

commit v5 on v4

--- a/solution.py
+++ b/solution.py
@@ -258,7 +258,7 @@
             device_id={"blk": p}, device_id_type=MESH,
         ).start()
 
-    order = [(dx, dy, dc) for dc in (1, 0) for dx in (2, 1, 3, 0) for dy in FAR if dx or dy or dc]
+    order = [(dx, dy, dc) for dc in (1, 0) for dx in (2, 1, 3, 0) for dy in (4, 0, 3, 7, 5, 1, 2, 6) if dx or dy or dc]
     ready = []
     for step, (dx, dy, dc) in enumerate(order):
         p = xs[dx] + ys[dy] + cs[dc]
@@ -321,13 +321,15 @@
         ]
         return jnp.concatenate(parts, axis=0)
 
-    def finish(slot, m):
+    def finish(slot, m, sends):
         for b in range(2):
             base, j = b * 64, (2 * m + b) * 4
             inw[slot, pl.ds(base, 8, stride=8), :] = both(j)
             inw[slot, pl.ds(base + 7, 8, stride=8), :] = both(j + 1)
             ins[slot, base:base + 8, :] = both(j + 2)
             ins[slot, base + 56:base + 64, :] = both(j + 3)
+        for d in sends:
+            level_copy(lax.rem(z + d, NZ)).start()
         wide_w, wide_s = jnp.transpose(inw[slot, :LANES]), jnp.transpose(ins[slot, :LANES])
         for h in range(2):
             k = m + 4 * h
@@ -348,11 +350,9 @@
 
     waiting = ()
     for slot, (o, nexts) in enumerate(((0, (4,)), (3, (3, 7)), (1, (5, 1)), (2, (2, 6)))):
-        finish(slot, lax.rem(z + o, 4))
+        finish(slot, lax.rem(z + o, 4), waiting)
         if slot == 0:
             lrecv[z] = lev[z]
-        for d in waiting:
-            level_copy(lax.rem(z + d, NZ)).start()
         waiting = nexts
     for d in waiting:
         level_copy(lax.rem(z + d, NZ)).start()
@@ -407,8 +407,8 @@
         q = (y + jnp.where(y >= 0.0, 0.5, -0.5)).astype(I32)
         tsend[k] = jnp.bitwise_or(jnp.left_shift(q[:ROWS // 2], 16), jnp.bitwise_and(q[ROWS // 2:], 65535))
         ssend[k] = unit
+        peak_copy(k).start()
         ret_copy(k).start()
-        peak_copy(k).start()
 
     def emit(k, t):
         at = pl.ds(pl.multiple_of(k * LANES, LANES), LANES)

time: 44.9 us -> 44.6 us (level)
  no operation moved by 1% of the time
where the time goes in v5:
time: 44.6 us; the launch traced here: 44.4 us
  Pallas kernels  43.7 us (98%)
  local copies, waits for them, and re-layouts  0.75 us (2%)
    pallas_call x1, Pallas kernels, shards(): pl.pallas_call(kernel, out_shape=pltpu.VMEM((FL, DIRS, PTS), F32), in_spe...  43.7 us

profile of v5, /device:TPU:8, one launch (start us, length us, event | category | flops | bytes accessed | tf_op | source)
XLA Modules:
  0.0 44.4 jit_solution(791512153700041877)
XLA Ops:
  0.0 43.7 %shard_map.109 = f32[4,24,1024]{2,1,0:T(8,128)S(1)} custom-call(f32[4,24,1024]{2,1,0:T(8,128)} %field_hbm.1, f32[8,128]{1,0:T(8,128)} %bitcast.5, f32[2,1024]{1,0:T(2,128)} %cur_hbm.1, f32[2,1024]{1,0:T(2,128)} %slope_hbm.1, f32[2,1024]{1,0:T(2,128)} %wind_hbm.1, s32[8,128]{1,0:T(8,128)} %bitcast.6, s32[1,64]{1,0:T(1,128)} %bitcast.7, s32[1,64]{1,0:T(1,128)} %bitcast.8, ...), custom_call_target="tpu_custom_call" | custom-call | tf_op jit(solution)/shard_map/pallas_call | solution.py:438
  43.7 0.7 %copy.13 = f32[4,24,1024]{2,1,0:T(8,128)} copy(f32[4,24,1024]{2,1,0:T(8,128)S(1)} %shard_map.109) | data formatting | bytes 786432

commit v6 on v5

--- a/solution.py
+++ b/solution.py
@@ -83,10 +83,11 @@
     plane = [(dx, dc) for dx in (2, 1, 3, 0) for dc in (1, 0) if dx or dc]
 
     for d in FAR[:-1]:
-        for at in ({"blk": xs[0] + ys[d] + cs[0]}, {"spec": lax.rem(z + d, NZ)}):
-            pl.semaphore_signal(barrier, inc=1, device_id=at, device_id_type=MESH)
+        pl.semaphore_signal(barrier, inc=1, device_id={"blk": xs[0] + ys[d] + cs[0]}, device_id_type=MESH)
     for dx, dc in plane:
         pl.semaphore_signal(barrier, inc=1, device_id={"blk": xs[dx] + ys[0] + cs[dc]}, device_id_type=MESH)
+    for d in FAR[:-1]:
+        pl.semaphore_signal(barrier, inc=1, device_id={"spec": lax.rem(z + d, NZ)}, device_id_type=MESH)
 
     small = [
         pltpu.make_async_copy(src, dst, op_sem.at[i]) for i, (src, dst) in enumerate((

time: 44.6 us -> 44.6 us (level)
  no operation moved by 1% of the time
where the time goes in v6:
time: 44.6 us; the launch traced here: 44.5 us
  Pallas kernels  43.7 us (98%)
  local copies, waits for them, and re-layouts  0.75 us (2%)
    pallas_call x1, Pallas kernels, shards(): pl.pallas_call(kernel, out_shape=pltpu.VMEM((FL, DIRS, PTS), F32), in_spe...  43.7 us

profile of v6, /device:TPU:8, one launch (start us, length us, event | category | flops | bytes accessed | tf_op | source)
XLA Modules:
  0.0 44.5 jit_solution(13102853376599847734)
XLA Ops:
  0.0 43.7 %shard_map.109 = f32[4,24,1024]{2,1,0:T(8,128)S(1)} custom-call(f32[4,24,1024]{2,1,0:T(8,128)} %field_hbm.1, f32[8,128]{1,0:T(8,128)} %bitcast.5, f32[2,1024]{1,0:T(2,128)} %cur_hbm.1, f32[2,1024]{1,0:T(2,128)} %slope_hbm.1, f32[2,1024]{1,0:T(2,128)} %wind_hbm.1, s32[8,128]{1,0:T(8,128)} %bitcast.6, s32[1,64]{1,0:T(1,128)} %bitcast.7, s32[1,64]{1,0:T(1,128)} %bitcast.8, ...), custom_call_target="tpu_custom_call" | custom-call | tf_op jit(solution)/shard_map/pallas_call | solution.py:439
  43.7 0.7 %copy.13 = f32[4,24,1024]{2,1,0:T(8,128)} copy(f32[4,24,1024]{2,1,0:T(8,128)S(1)} %shard_map.109) | data formatting | bytes 786432

commit v7 on v5

--- a/solution.py
+++ b/solution.py
@@ -359,14 +359,16 @@
     for k in range(NCH):
         g1[k] = mv[k] * g1[k]
 
-    for o in range(1, NZ):
+    mv[z] = lrecv[z].astype(F32)
+    for o in (1, 7, 2, 6, 3, 5, 4):
         k = lax.rem(z + o, NZ)
         pltpu.make_async_remote_copy(
             src_ref=lev.at[k], dst_ref=lrecv.at[k], send_sem=l_send.at[k], recv_sem=l_recv.at[k],
             device_id={"spec": k}, device_id_type=MESH,
         ).wait()
-
-    levels = lrecv[...].reshape(FREQS * DIRS, LANES).astype(F32)
+        mv[k] = lrecv[k].astype(F32)
+
+    levels = mv[...].reshape(FREQS * DIRS, LANES)
     level_f = to_freq_form(levels).astype(BF16)
     both_shifted = dot(kf[...], level_f)
     shifted = [to_angle_form(from_freq_form(both_shifted[256 * s:256 * s + 256])).astype(BF16) for s in range(2)]

time: 44.6 us -> 44.6 us (level)
  no operation moved by 1% of the time
where the time goes in v7:
time: 44.6 us; the launch traced here: 44.5 us
  Pallas kernels  43.7 us (98%)
  local copies, waits for them, and re-layouts  0.75 us (2%)
    pallas_call x1, Pallas kernels, shards(): pl.pallas_call(kernel, out_shape=pltpu.VMEM((FL, DIRS, PTS), F32), in_spe...  43.7 us

profile of v7, /device:TPU:8, one launch (start us, length us, event | category | flops | bytes accessed | tf_op | source)
XLA Modules:
  0.0 44.5 jit_solution(7829374169914434196)
XLA Ops:
  0.0 43.7 %shard_map.109 = f32[4,24,1024]{2,1,0:T(8,128)S(1)} custom-call(f32[4,24,1024]{2,1,0:T(8,128)} %field_hbm.1, f32[8,128]{1,0:T(8,128)} %bitcast.5, f32[2,1024]{1,0:T(2,128)} %cur_hbm.1, f32[2,1024]{1,0:T(2,128)} %slope_hbm.1, f32[2,1024]{1,0:T(2,128)} %wind_hbm.1, s32[8,128]{1,0:T(8,128)} %bitcast.6, s32[1,64]{1,0:T(1,128)} %bitcast.7, s32[1,64]{1,0:T(1,128)} %bitcast.8, ...), custom_call_target="tpu_custom_call" | custom-call | tf_op jit(solution)/shard_map/pallas_call | solution.py:440
  43.7 0.7 %copy.13 = f32[4,24,1024]{2,1,0:T(8,128)} copy(f32[4,24,1024]{2,1,0:T(8,128)S(1)} %shard_map.109) | data formatting | bytes 786432
